TPU v7x, 512 devices: a whole 4x8x8 slice. The times are simulated.
512 devices in a mesh: gr: 16 (over y, core), gc: 32 (over z, x).
Axes of the slice: x: 4, y: 8, z: 8, core: 2. Of those that a mesh axis runs over, the one named last changes fastest.
Arguments:
- weights: bfloat16 [8192, 8192], P('gc', 'gr'), may hold values from 0.049804688 to 5
- in_pattern: int32 [64, 64], P('gc', 'gr'), may hold values from 0 to 1, as said below
- out_pattern: int32 [64, 64], P('gc', 'gr'), may hold values from 0 to 1, as said below
Outputs:
- next_matrix: bfloat16 [8192, 8192], P('gc', 'gr')
Inputs may be any that keep to these rules, and one draw needn't show every extreme that they name: `in_pattern`: 0 or 1 a block; every diagonal block is 1; each aligned tile of 2 block rows by 4 block columns holds at most 4 ones, and one such tile holds exactly 4. `out_pattern`: 0 or 1 a block; every diagonal block is 1.
All inputs are finite; a program needn't handle non-finite values.
Results may differ from a plain program's by a relative error of at most 0.0055.
Values may be sent and summed in bfloat16 or wider, within the bound.
A program may use at most 128 MiB of HBM per device.

v0:
```python
import jax
import jax.numpy as jnp
from jax import lax
from jax.sharding import PartitionSpec as P


def mask_blocks(local_tile, block_flags, block_size):
    blk_rows, blk_cols = block_flags.shape
    shaped = local_tile.reshape(blk_rows, block_size, blk_cols, block_size)
    return (shaped * block_flags[:, None, :, None].astype(local_tile.dtype)).reshape(
        local_tile.shape
    )


def shards(weights, in_pattern, out_pattern):
    blk_rows, blk_cols = in_pattern.shape
    local_rows, local_cols = weights.shape
    block_size = local_rows // blk_rows
    grid_cols = lax.axis_size("gc")
    order_size = local_rows * grid_cols
    masked = mask_blocks(weights, in_pattern, block_size)
    column_part = jnp.sum(masked, axis=0, dtype=jnp.float32)
    input_total = lax.psum(column_part, "gc")
    inverse_local = 1.0 / input_total
    source = (masked.astype(jnp.float32) * inverse_local[None, :]).astype(jnp.bfloat16)
    row_panel = lax.all_gather(source, "gr", axis=1, tiled=True)
    product = jnp.dot(
        row_panel,
        lax.all_gather(source, "gc", axis=0, tiled=True),
        preferred_element_type=jnp.float32,
    )
    pruned = product.reshape(blk_rows, block_size, blk_cols, block_size) * out_pattern[
        :, None, :, None
    ].astype(jnp.float32)
    inflated = (pruned * pruned).reshape(local_rows, local_cols)
    output_total = lax.psum(jnp.sum(inflated, axis=0), "gc")
    return (inflated / output_total[None, :] * float(order_size)).astype(jnp.bfloat16)


def solution(mesh):
    in_specs = (P("gc", "gr"), P("gc", "gr"), P("gc", "gr"))
    out_specs = P("gc", "gr")
    return jax.shard_map(shards, mesh=mesh, in_specs=in_specs, out_specs=out_specs, check_vma=False)
```

profile of v0, /device:TPU:8, one launch (start us, length us, event | category | flops | bytes accessed | tf_op | source)
XLA Modules:
  0.0 322.3 jit_solution(4489098773115387270)
XLA Ops:
  6.5 0.0 all-gather.3.cloned.1.call-start
  6.5 0.7 convert_element_type.18
  7.2 0.1 mul.40
  7.4 1.0 convert_reduce_fusion
  8.4 80.8 %psum.14 = f32[512]{0:T(512)S(1)} all-reduce(f32[512]{0:T(512)S(1)} %convert_reduce_fusion), channel_id=1, replica_groups=mesh['gr'=16,'gc'=32] {'gc'}, use_global_device_ids=true, to_apply=%region_1.0 | all-reduce | flops 512 | bytes 4096 | tf_op jit(solution)/shard_map/psum | solution.py:23
  89.3 1.7 fusion.1
  91.0 0.0 all-gather.3.cloned.1.call-update
  91.0 0.0 all-gather.5.cloned.1.call-start
  91.1 0.7 all-gather.5.cloned.1.call-update
  91.8 0.7 convert_element_type.21
  92.5 36.8 %all-gather.3.cloned.1.call-done = bf16[256,8192]{1,0:T(8,128)(2,1)} async-done(((bf16[256,512]{1,0:T(8,128)(2,1)}), bf16[256,8192]{1,0:T(8,128)(2,1)}) %all-gather.3.cloned.1.call-update) | async-done | bytes 4194320 | tf_op jit(solution)/shard_map/all_gather | solution.py:26
  129.2 107.1 %all-gather.5.cloned.1.call-done = bf16[8192,512]{1,0:T(8,128)(2,1)} async-done(((bf16[256,512]{1,0:T(8,128)(2,1)}), bf16[8192,512]{1,0:T(8,128)(2,1)}) %all-gather.5.cloned.1.call-update) | async-done | bytes 8388624 | tf_op jit(solution)/shard_map/all_gather | solution.py:29
  236.3 0.1 mul.45
  236.5 7.0 %fusion.2 = (f32[512]{0:T(512)S(1)}, f32[256,512]{1,0:T(8,128)S(1)}) fusion(f32[32,8,4,128]{3,2,1,0:T(4,128)S(1)} %bitcast.16, bf16[256,8192]{1,0:T(8,128)(2,1)} %all-gather.3.cloned.1.call-done, bf16[8192,512]{1,0:T(8,128)(2,1)} %all-gather.5.cloned.1.call-done), kind=kOutput, calls=%fused_computation.8 | convolution fusion | flops 2147876352 | bytes 13633536 | tf_op jit(solution)/shard_map/dot_general | solution.py:27
  243.5 71.2 %psum.15 = f32[512]{0:T(512)S(1)} all-reduce(f32[512]{0:T(512)S(1)} %get-tuple-element.5), channel_id=1, replica_groups=mesh['gr'=16,'gc'=32] {'gc'}, use_global_device_ids=true, to_apply=%region_3.0 | all-reduce | flops 512 | bytes 4096 | tf_op jit(solution)/shard_map/psum | solution.py:36
  314.7 0.8 multiply_convert_fusion
  (1 shorter events, 0.0 us)
Async XLA Ops:
  6.5 122.7 %all-gather.3.cloned.1.call-start = ((), (), s32[]{:S(2)}) async-start(), calls=%async_computation | async-start | bytes 4456448 | tf_op jit(solution)/shard_map/all_gather | solution.py:26
  91.0 145.3 %all-gather.5.cloned.1.call-start = ((), (), s32[]{:S(2)}) async-start(), calls=%async_computation.1 | async-start | bytes 8650752 | tf_op jit(solution)/shard_map/all_gather | solution.py:29
Sparse Core Ops, SparseCore 0:
  91.1 38.0 all-gather.2
  132.4 103.9 all-gather.4
where the time goes:
time: 323 us; the launch traced here: 322 us
  blocking collectives  152 us (47%)
  waiting for transfers between devices  145 us (45%)
  between operations  13.4 us (4%)
  matrix products  7 us (2%)
  other arithmetic  4.92 us (2%)
    all_gather x1, waiting for transfers between devices, shards(): lax.all_gather(source, 'gc', axis=0, tiled=True)  107 us
    psum x1, blocking collectives, shards(): input_total = lax.psum(column_part, 'gc')  80.8 us
    psum x1, blocking collectives, shards(): output_total = lax.psum(jnp.sum(inflated, axis=0), 'gc')  71.2 us
    all_gather x1, waiting for transfers between devices, shards(): row_panel = lax.all_gather(source, 'gr', axis=1, tiled=True)  36.8 us
    dot_general x1, matrix products, shards(): jnp.dot(row_panel, lax.all_gather(source, 'gc', axis=0, tiled=True), pref...  7 us
  transfers between devices with their start and end apart: 2, of which 2 were waited for; matrix products, arithmetic and copies ran while one was open for 0% of the time, Pallas kernels for 0%

commit v1 on v0

v1 whole, which is shorter than its diff:
```python
import functools

import jax
import jax.numpy as jnp
from jax import lax
from jax.experimental import pallas as pl
from jax.experimental.pallas import tpu as pltpu
from jax.sharding import PartitionSpec as P

MESH = pl.DeviceIdType.MESH
X = 4
CORES = 2
CAP = 4
SUM_SCALE = float(1 << 14)
CODE_ROW = 4


def kernel(
    gc, gr, blk,
    w_ref, ip_ref, op_ref, o_ref,
    bbuf, abuf, bdense, adense, acc, meta_b, meta_a, totals,
    z_recv, x_recv, y_recv, sib_recv, small_recv, send_sem,
):
    br, bc = ip_ref.shape
    z_chips, y_chips = gc // X, gr // CORES
    tile = CAP * blk
    part = tile // 2
    half = part // 2
    f32, bf16 = jnp.float32, jnp.bfloat16

    me = lax.axis_index("gc")
    mine = lax.axis_index("gr")
    x, z = lax.rem(me, X), lax.div(me, X)
    core, y = lax.rem(mine, CORES), lax.div(mine, CORES)

    def at(dx, dz):
        return lax.rem(z + dz + z_chips, z_chips) * X + lax.rem(x + dx + X, X)

    def at_y(dy, c):
        return lax.rem(y + dy + y_chips, y_chips) * CORES + c

    barrier = pltpu.get_barrier_semaphore()

    @pl.loop(1, gc)
    def _(j):
        pl.semaphore_signal(barrier, inc=1, device_id={"gc": lax.rem(me + j, gc)}, device_id_type=MESH)

    @pl.loop(1, gr)
    def _(j):
        pl.semaphore_signal(barrier, inc=1, device_id={"gr": lax.rem(mine + j, gr)}, device_id_type=MESH)

    def rows(origin):
        return pl.multiple_of(origin * tile, tile)

    spots = br * bc
    on = [(ip_ref[p // bc, p % bc] > 0).astype(jnp.int32) for p in range(spots)]
    spare = CAP - sum(on)
    count = jnp.int32(0)
    place = [jnp.int32(0)] * CAP
    for p in range(spots):
        filler = jnp.logical_and(on[p] == 0, spare > 0).astype(jnp.int32)
        spare = spare - filler
        used = on[p] + filler
        for s in range(CAP):
            place[s] = place[s] + jnp.where(count == s, used, 0) * p
        count = count + used

    def reach(p):
        return range(max(0, p - (spots - CAP)), min(CAP - 1, p) + 1)

    def block_of(p):
        r, c = p // bc, p % bc
        return w_ref[r * blk : (r + 1) * blk, c * blk : (c + 1) * blk]

    for s in range(CAP):
        slot = jnp.zeros((blk, blk), f32)
        for p in range(s, s + spots - CAP + 1):
            slot += block_of(p).astype(f32) * (jnp.where(place[s] == p, on[p], 0).astype(f32))
        bbuf[pl.ds(rows(me) + s * blk, blk), :] = slot.astype(bf16)

    for c in range(bc):
        total = jnp.zeros((1, blk), f32)
        for r in range(br):
            block = block_of(r * bc + c).astype(f32)
            total += jnp.sum(block, axis=0, keepdims=True) * on[r * bc + c].astype(f32)
        row = (total * SUM_SCALE).astype(jnp.int32)
        meta_b[me, c : c + 1, :] = row
        meta_a[mine, c : c + 1, :] = row
    for s in range(CAP):
        row = jnp.full((1, blk), 0, jnp.int32) + place[s]
        meta_b[me, CODE_ROW + s : CODE_ROW + s + 1, :] = row
        meta_a[mine, CODE_ROW + s : CODE_ROW + s + 1, :] = row

    pl.semaphore_wait(barrier, gc + gr - 2)

    P_ROWS, Q_ROWS, HALF = 0, part, half

    def b_copy(origin, first, size, dst, recv):
        ref = bbuf.at[pl.ds(rows(origin) + first, size), :]
        return pltpu.make_async_remote_copy(
            src_ref=ref, dst_ref=ref, send_sem=send_sem.at[0], recv_sem=recv,
            device_id={"gc": dst}, device_id_type=MESH,
        )

    z_half = z_chips // 2
    Q = X

    def z_copy(s, h, item):
        sign = 1 - 2 * s
        origin = at(0 if item == Q else item, -sign * (h - 1))
        first = Q_ROWS if item == Q else P_ROWS
        size = part
        if h == z_half:
            first, size = first + s * HALF, HALF
        return b_copy(origin, first, size, at(0, sign), z_recv.at[s, h - 1, item])

    PX = z_chips

    def x_copy(d, k, item):
        sign = 1 - 2 * d
        origin = at(-sign * (k - 1), 0 if item == PX else item)
        first = P_ROWS if item == PX else Q_ROWS
        size = part
        if k == X // 2:
            first, size = first + d * HALF, HALF
        return b_copy(origin, first, size, at(sign, 0), x_recv.at[d, k - 1, item])

    def small(ref, index, axis, peer, k):
        return pltpu.make_async_remote_copy(
            src_ref=ref.at[index], dst_ref=ref.at[index], send_sem=send_sem.at[k], recv_sem=small_recv.at[k - 2],
            device_id={axis: peer}, device_id_type=MESH,
        )

    def all_small(ref, n, axis, k):
        view = ref.at[pl.ds(0, n - 1)]
        return pltpu.make_async_remote_copy(
            src_ref=view, dst_ref=view, send_sem=send_sem.at[k], recv_sem=small_recv.at[k - 2],
            device_id={axis: 0}, device_id_type=MESH,
        )

    y_half = y_chips // 2

    def a_copy(origin, first, size, dst, recv):
        ref = abuf.at[pl.ds(rows(origin) + first, size), :]
        return pltpu.make_async_remote_copy(
            src_ref=ref, dst_ref=ref, send_sem=send_sem.at[1], recv_sem=recv,
            device_id={"gr": dst}, device_id_type=MESH,
        )

    def y_copy(s, h):
        sign = 1 - 2 * s
        first, size = (s * part, part) if h == y_half else (0, tile)
        return a_copy(at_y(-sign * (h - 1), core), first, size, at_y(sign, core), y_recv.at[s, h - 1])

    def sib_copy(dy, c):
        return a_copy(at_y(dy, c), 0, tile, at_y(0, 1 - c), sib_recv.at[dy % y_chips])

    for s in range(2):
        z_copy(s, 1, Q).start()
    for d in range(2):
        x_copy(d, 1, PX).start()
    for s in range(2):
        z_copy(s, 1, 0).start()
    for d in range(2):
        x_copy(d, 1, 0).start()

    @pl.loop(1, gc)
    def _(j):
        small(meta_b, me, "gc", lax.rem(me + j, gc), 2).start()

    @pl.loop(1, gr)
    def _(j):
        small(meta_a, mine, "gr", lax.rem(mine + j, gr), 3).start()

    for d in range(2):
        x_copy(d, 1, PX).wait_recv()
        x_copy(d, 2, PX).start()
        for s in range(2):
            z_copy(s, 1, (X - 1) if d == 0 else 1).start()
    for d in range(2):
        x_copy(d, 2, PX).wait_recv()
    for s in range(2):
        z_copy(s, 1, X // 2).start()

    all_small(meta_b, gc, "gc", 2).wait_recv()
    input_total = jnp.sum(meta_b[...], axis=0).astype(f32) * (1.0 / SUM_SCALE)
    inverse = 1.0 / input_total
    for s in range(CAP):
        factor = jnp.zeros((1, blk), f32)
        for c in range(bc):
            factor += inverse[c : c + 1, :] * (lax.rem(place[s], bc) == c).astype(f32)
        block = bbuf[pl.ds(rows(me) + s * blk, blk), :].astype(f32)
        abuf[pl.ds(rows(mine) + s * blk, blk), :] = (block * factor).astype(bf16)
    for s in range(2):
        y_copy(s, 1).start()
    sib_copy(0, core).start()

    for d in range(2):
        x_copy(d, 1, 0).wait_recv()
        x_copy(d, 2, 0).start()

    for h in range(1, z_half + 1):
        last = h == z_half
        for s in range(2):
            z_copy(s, h, Q).wait_recv()
            if not last:
                z_copy(s, h + 1, Q).start()
                for d in range(2):
                    x_copy(d, 1, (-h if s == 0 else h) % z_chips).start()
        if last:
            for d in range(2):
                x_copy(d, 1, h).start()
        for item in (0, 1, X - 1, X // 2):
            for s in range(2):
                z_copy(s, h, item).wait_recv()
                if not last:
                    z_copy(s, h + 1, item).start()
        if h <= y_half:
            for s in range(2):
                y_copy(s, h).wait_recv()
                if h < y_half:
                    y_copy(s, h + 1).start()
                    sib_copy(-h if s == 0 else h, core).start()
            if h == y_half:
                sib_copy(h, core).start()
        for dz in (h % z_chips, -h % z_chips) if not last else (h,):
            for d in range(2):
                x_copy(d, 1, dz).wait_recv()
                x_copy(d, 2, dz).start()
    for dz in range(z_chips):
        for d in range(2):
            x_copy(d, 2, dz).wait_recv()
    for dy in range(y_chips):
        sib_copy(dy, 1 - core).wait_recv()

    all_small(meta_a, gr, "gr", 3).wait_recv()

    def spread(t, meta, buf, dst, r_base):
        slots = [buf[pl.ds(rows(t) + s * blk, blk), :] for s in range(CAP)]
        places = [meta[t, CODE_ROW + s : CODE_ROW + s + 1, :] for s in range(CAP)]
        for p in range(spots):
            block = sum(slots[s] * (places[s] == p).astype(f32).astype(bf16) for s in reach(p))
            r, c = p // bc, p % bc
            dst[pl.ds(r_base + r * blk, blk), c * blk : (c + 1) * blk] = block

    per = (bc * blk) // (br * blk)

    @pl.loop(0, gr)
    def _(t):
        spread(t, meta_a, abuf, adense.at[t], 0)
        for i in range(per):
            spread(t * per + i, meta_b, bbuf, bdense.at[t], i * br * blk)

    acc[...] = jnp.zeros_like(acc)

    @pl.loop(0, gr)
    def _(t):
        acc[...] += jnp.dot(adense[t], bdense[t], preferred_element_type=f32)

    for c in range(bc):
        total = jnp.zeros((1, blk), f32)
        for r in range(br):
            block = acc[r * blk : (r + 1) * blk, c * blk : (c + 1) * blk] * op_ref[r, c].astype(f32)
            block = block * block
            acc[r * blk : (r + 1) * blk, c * blk : (c + 1) * blk] = block
            total += jnp.sum(block, axis=0, keepdims=True)
        totals[me, c : c + 1, :] = total

    @pl.loop(1, gc)
    def _(j):
        small(totals, me, "gc", lax.rem(me + j, gc), 4).start()

    all_small(totals, gc, "gc", 4).wait_recv()
    output_total = jnp.sum(totals[...], axis=0)
    factor = float(gc * br * blk) / output_total
    for c in range(bc):
        o_ref[:, c * blk : (c + 1) * blk] = (acc[:, c * blk : (c + 1) * blk] * factor[c : c + 1, :]).astype(bf16)

    b_copy(0, 0, (gc - 1) * tile, 0, z_recv.at[0, 0, 0]).wait_send()
    a_copy(0, 0, (gr - 1) * tile, 0, y_recv.at[0, 0]).wait_send()
    all_small(meta_b, gc, "gc", 2).wait_send()
    all_small(meta_a, gr, "gr", 3).wait_send()
    all_small(totals, gc, "gc", 4).wait_send()


def solution(mesh):
    gc, gr = mesh.shape["gc"], mesh.shape["gr"]

    def shards(weights, in_pattern, out_pattern):
        rows, cols = weights.shape
        br, bc = in_pattern.shape
        blk = rows // br
        tile = CAP * blk
        z_chips, y_chips = gc // X, gr // CORES
        dma = pltpu.SemaphoreType.DMA
        return pl.pallas_call(
            functools.partial(kernel, gc, gr, blk),
            out_shape=jax.ShapeDtypeStruct(weights.shape, weights.dtype),
            in_specs=[
                pl.BlockSpec(memory_space=pltpu.VMEM),
                pl.BlockSpec(memory_space=pltpu.SMEM),
                pl.BlockSpec(memory_space=pltpu.SMEM),
            ],
            out_specs=pl.BlockSpec(memory_space=pltpu.VMEM),
            scratch_shapes=[
                pltpu.VMEM((gc * tile, blk), jnp.bfloat16),
                pltpu.VMEM((gr * tile, blk), jnp.bfloat16),
                pltpu.VMEM((gr, cols, cols), jnp.bfloat16),
                pltpu.VMEM((gr, rows, cols), jnp.bfloat16),
                pltpu.VMEM((rows, cols), jnp.float32),
                pltpu.VMEM((gc, 8, blk), jnp.int32),
                pltpu.VMEM((gr, 8, blk), jnp.int32),
                pltpu.VMEM((gc, bc, blk), jnp.float32),
                dma((2, z_chips // 2, X + 1)),
                dma((2, X // 2, z_chips + 1)),
                dma((2, y_chips // 2)),
                dma((y_chips,)),
                dma((3,)),
                dma((5,)),
            ],
            compiler_params=pltpu.CompilerParams(
                collective_id=0, has_side_effects=True, vmem_limit_bytes=48 << 20
            ),
        )(weights, in_pattern, out_pattern)

    spec = P("gc", "gr")
    return jax.shard_map(shards, mesh=mesh, in_specs=(spec, spec, spec), out_specs=spec, check_vma=False)
```

time: 323 us -> 72.9 us (0.23)
  the two profiles are of different devices: /device:TPU:8 before, /device:TPU:24 now
where the time goes in v1:
time: 72.9 us; the launch traced here: 72.7 us
  Pallas kernels  69.7 us (96%)
  local copies, waits for them, and re-layouts  3.01 us (4%)
    pallas_call x1, Pallas kernels, shards(): pl.pallas_call(functools.partial(kernel, gc, gr, blk), out_shape=jax.Shap...  69.7 us
    unnamed x7, local copies, waits for them, and re-layouts  3.01 us

profile of v1, /device:TPU:24, one launch (start us, length us, event | category | flops | bytes accessed | tf_op | source)
XLA Modules:
  0.0 72.7 jit_solution(17914077255346207732)
XLA Ops:
  0.0 0.0 copy-start
  0.0 0.9 %copy-done = bf16[256,512]{1,0:T(8,128)(2,1)S(1)} copy-done((bf16[256,512]{1,0:T(8,128)(2,1)S(1)}, bf16[256,512]{1,0:T(8,128)(2,1)}, u32[]{:S(2)}) %copy-start) | copy-done | bytes 262168
  1.0 0.0 copy-start.1
  1.0 0.7 copy-done.1
  1.6 0.0 copy-start.2
  1.6 0.7 copy-done.2
  2.3 69.7 %shard_map.37 = bf16[256,512]{1,0:T(8,128)(2,1)S(1)} custom-call(bf16[256,512]{1,0:T(8,128)(2,1)S(1)} %copy-done, s32[2,4]{1,0:T(2,128)S(1)} %copy-done.1, s32[2,4]{1,0:T(2,128)S(1)} %copy-done.2), custom_call_target="tpu_custom_call" | custom-call | tf_op jit(solution)/shard_map/pallas_call | solution.py:296
  72.0 0.7 copy.5
Async XLA Ops:
  0.0 0.9 %copy-start = (bf16[256,512]{1,0:T(8,128)(2,1)S(1)}, bf16[256,512]{1,0:T(8,128)(2,1)}, u32[]{:S(2)}) copy-start(bf16[256,512]{1,0:T(8,128)(2,1)} %w_ref.1) | copy-start | bytes 786436
  1.0 0.7 copy-start.1
  1.6 0.7 copy-start.2

commit v2 on v0

v2 whole, which is shorter than its diff:
```python
import functools

import jax
import jax.numpy as jnp
from jax import lax
from jax.experimental import pallas as pl
from jax.experimental.pallas import tpu as pltpu
from jax.sharding import PartitionSpec as P

MESH = pl.DeviceIdType.MESH
X = 4
CORES = 2
CAP = 4
CODE = 16
P_ROWS = 208


def kernel(
    gc, gr, blk,
    w_hbm, ip_hbm, op_hbm, o_ref,
    w_ref, ip_ref, op_ref, bbuf, abuf, bdense, adense, acc, x_sums, z_sums, inverses, totals,
    z_recv, x_recv, y_recv, sib_recv, small_recv, send_sem, local_sem,
):
    br, bc = ip_ref.shape
    z_chips, y_chips = gc // X, gr // CORES
    x_half, y_half, z_half = X // 2, y_chips // 2, z_chips // 2
    data = CAP * blk
    tile = data + CODE
    f32, bf16 = jnp.float32, jnp.bfloat16

    me = lax.axis_index("gc")
    mine = lax.axis_index("gr")
    x, z = lax.rem(me, X), lax.div(me, X)
    core, y = lax.rem(mine, CORES), lax.div(mine, CORES)

    def at(dx, dz):
        return lax.rem(z + (dz + z_chips), z_chips) * X + lax.rem(x + (dx + X), X)

    def at_y(dy, c):
        return lax.rem(y + (dy + y_chips), y_chips) * CORES + c

    def rows(origin, first=0):
        return pl.multiple_of(origin * tile + first, CODE)

    loads = [
        pltpu.make_async_copy(src, dst, local_sem.at[i])
        for i, (src, dst) in enumerate(((ip_hbm, ip_ref), (w_hbm, w_ref), (op_hbm, op_ref)))
    ]
    for load in loads:
        load.start()
    barrier = pltpu.get_barrier_semaphore()
    x_peers = [{"gc": at(i, 0)} for i in range(1, X)]
    z_peers = [{"gc": at(0, i)} for i in range(1, z_chips)]
    greeted = x_peers + z_peers + [{"gr": at_y(1, core)}, {"gr": at_y(-1, core)}, {"gr": at_y(0, 1 - core)}]
    for peer in greeted:
        pl.semaphore_signal(barrier, inc=1, device_id=peer, device_id_type=MESH)
    for load in loads:
        load.wait()

    spots = br * bc
    on = [(ip_ref[p // bc, p % bc] > 0).astype(jnp.int32) for p in range(spots)]
    spare = CAP - sum(on)
    count = jnp.int32(0)
    place = [jnp.int32(0)] * CAP
    for p in range(spots):
        filler = jnp.logical_and(on[p] == 0, spare > 0).astype(jnp.int32)
        spare = spare - filler
        used = on[p] + filler
        for s in range(CAP):
            place[s] = place[s] + jnp.where(count == s, used, 0) * p
        count = count + used

    def reach(p):
        return range(max(0, p - (spots - CAP)), min(CAP - 1, p) + 1)

    def block_of(p):
        r, c = p // bc, p % bc
        return w_ref[r * blk : (r + 1) * blk, c * blk : (c + 1) * blk]

    for c in range(bc):
        total = jnp.zeros((1, blk), f32)
        for r in range(br):
            block = block_of(r * bc + c).astype(f32)
            total += jnp.sum(block, axis=0, keepdims=True) * on[r * bc + c].astype(f32)
        x_sums[x, c : c + 1, :] = total
    code_row = lax.broadcasted_iota(jnp.int32, (CODE, blk), 0)
    codes = jnp.zeros((CODE, blk), f32)
    for s in range(CAP):
        slot = jnp.zeros((blk, blk), f32)
        for p in range(s, s + spots - CAP + 1):
            slot += block_of(p).astype(f32) * (jnp.where(place[s] == p, on[p], 0).astype(f32))
        slot = slot.astype(bf16)
        bbuf[pl.ds(rows(me, s * blk), blk), :] = slot
        abuf[pl.ds(rows(mine, s * blk), blk), :] = slot
        codes = jnp.where(code_row == s, place[s].astype(f32), codes)
    codes = codes.astype(bf16)
    bbuf[pl.ds(rows(me, data), CODE), :] = codes
    abuf[pl.ds(rows(mine, data), CODE), :] = codes

    pl.semaphore_wait(barrier, len(greeted))

    def cut(first, size, which):
        low = (size // 2 + CODE - 1) // CODE * CODE
        return (first, low) if which == 0 else (first + low, size - low)

    P_PART, Q_PART = (0, P_ROWS), (P_ROWS, tile - P_ROWS)

    def b_copy(origin, part, dst, recv):
        ref = bbuf.at[pl.ds(rows(origin, part[0]), part[1]), :]
        return pltpu.make_async_remote_copy(
            src_ref=ref, dst_ref=ref, send_sem=send_sem.at[0], recv_sem=recv,
            device_id={"gc": dst}, device_id_type=MESH,
        )

    Q = X

    def z_copy(s, h, item):
        sign = 1 - 2 * s
        part = Q_PART if item == Q else P_PART
        if h == z_half:
            part = cut(*part, s)
        origin = at(0 if item == Q else item, -sign * (h - 1))
        return b_copy(origin, part, at(0, sign), z_recv.at[s, h - 1, item])

    PX = z_chips

    def x_copy(d, k, item):
        sign = 1 - 2 * d
        part = P_PART if item == PX else Q_PART
        if k == x_half:
            part = cut(*part, d)
        origin = at(-sign * (k - 1), 0 if item == PX else item)
        return b_copy(origin, part, at(sign, 0), x_recv.at[d, k - 1, item])

    def a_copy(origin, part, dst, recv):
        ref = abuf.at[pl.ds(rows(origin, part[0]), part[1]), :]
        return pltpu.make_async_remote_copy(
            src_ref=ref, dst_ref=ref, send_sem=send_sem.at[1], recv_sem=recv,
            device_id={"gr": dst}, device_id_type=MESH,
        )

    def y_copy(s, h, piece):
        sign = 1 - 2 * s
        return a_copy(at_y(-sign * (h - 1), core), cut(0, tile, piece), at_y(sign, core), y_recv.at[s, h - 1, piece])

    def sib_copy(dy, c):
        return a_copy(at_y(dy, c), (0, tile), at_y(0, 1 - c), sib_recv.at[dy % y_chips])

    def small(ref, index, peer, k):
        return pltpu.make_async_remote_copy(
            src_ref=ref.at[index], dst_ref=ref.at[index], send_sem=send_sem.at[k], recv_sem=small_recv.at[k - 2],
            device_id=peer, device_id_type=MESH,
        )

    def all_small(ref, n, peer, k):
        view = ref.at[pl.ds(0, n)]
        return pltpu.make_async_remote_copy(
            src_ref=view, dst_ref=view, send_sem=send_sem.at[k], recv_sem=small_recv.at[k - 2],
            device_id=peer, device_id_type=MESH,
        )

    X_SUMS, Z_SUMS, INVERSES, TOTALS = 2, 3, 4, 5

    def y_step(h):
        for piece in range(2):
            for s in range(2):
                if h < y_half or piece == s:
                    y_copy(s, h, piece).wait_recv()
                if h + 1 < y_half or (h < y_half and piece == s):
                    y_copy(s, h + 1, piece).start()
        for dy in (-h, h) if h < y_half else (h,):
            sib_copy(dy, core).start()

    def x_step(k, dz):
        for d in range(2):
            x_copy(d, k, dz).wait_recv()
            if k < x_half:
                x_copy(d, k + 1, dz).start()

    def z_step(h, item):
        for s in range(2):
            z_copy(s, h, item).wait_recv()
            if h < z_half:
                z_copy(s, h + 1, item).start()

    def spread(t, buf, dst, r_base, c_base, inverse=None):
        codes = buf[pl.ds(rows(t, data), CODE), :].astype(f32)
        places = [codes[s : s + 1, :] for s in range(CAP)]
        slots = [buf[pl.ds(rows(t, s * blk), blk), :] for s in range(CAP)]
        if inverse is not None:
            for s in range(CAP):
                factor = sum(
                    inverse[c : c + 1, :] * sum((places[s] == float(r * bc + c)).astype(f32) for r in range(br))
                    for c in range(bc)
                )
                slots[s] = (slots[s].astype(f32) * factor).astype(bf16)
        for p in range(spots):
            block = sum(slots[s] * (places[s] == float(p)).astype(f32).astype(bf16) for s in reach(p))
            r, c = p // bc, p % bc
            dst[pl.ds(r_base + r * blk, blk), pl.ds(c_base + c * blk, blk)] = block

    def left():
        per = X * br // bc

        @pl.loop(0, z_chips)
        def _(zz):
            for i in range(per):
                t = zz * per + i
                spread(t, abuf, adense.at[zz], 0, i * bc * blk, inverses[t])

    def quad(dz, first=False):
        zz = lax.rem(z + (dz + z_chips), z_chips)

        @pl.loop(0, X)
        def _(i):
            spread(zz * X + i, bbuf, bdense.at[zz], pl.multiple_of(i * (br * blk), blk), 0)

        term = jnp.dot(adense[zz], bdense[zz], preferred_element_type=f32)
        acc[...] = term if first else acc[...] + term

    for peer in x_peers:
        small(x_sums, x, peer, X_SUMS).start()
    for s in range(2):
        z_copy(s, 1, Q).start()
        x_copy(s, 1, PX).start()
    for piece in range(2):
        for s in range(2):
            y_copy(s, 1, piece).start()
    for s in range(2):
        z_copy(s, 1, 0).start()
        x_copy(s, 1, 0).start()
    sib_copy(0, core).start()

    all_small(x_sums, X - 1, x_peers[0], X_SUMS).wait_recv()
    z_sums[z] = jnp.sum(x_sums[...], axis=0)
    for peer in z_peers:
        small(z_sums, z, peer, Z_SUMS).start()
    for d in range(2):
        x_copy(d, 1, PX).wait_recv()
        x_copy(d, 2, PX).start()
        for s in range(2):
            z_copy(s, 1, (X - 1) if d == 0 else 1).start()
    for d in range(2):
        x_copy(d, 2, PX).wait_recv()
    for s in range(2):
        z_copy(s, 1, x_half).start()

    for h in range(1, z_half + 1):
        last = h == z_half
        for s in range(2):
            z_copy(s, h, Q).wait_recv()
            if not last:
                z_copy(s, h + 1, Q).start()
                for d in range(2):
                    x_copy(d, 1, (-h if s == 0 else h) % z_chips).start()
        if last:
            for d in range(2):
                x_copy(d, 1, h).start()
        if h == 1:
            x_step(1, 0)
        y_now = {1: (1,), 2: (2, 3)}.get(h, ())
        z_step(h, 0)
        if h == 1:
            all_small(z_sums, z_chips - 1, z_peers[0], Z_SUMS).wait_recv()
            inverses[mine] = 1.0 / jnp.sum(z_sums[...], axis=0)
        for i in y_now[:1]:
            y_step(i)
        if h == 3:
            y_step(4)
            for dy in range(y_chips):
                sib_copy(dy, 1 - core).wait_recv()
            for i in range(1, gr):
                small(inverses, mine, {"gr": lax.rem(mine + i, gr)}, INVERSES).start()
        z_step(h, 1)
        z_step(h, X - 1)
        if last:
            all_small(inverses, gr - 1, {"gr": 0}, INVERSES).wait_recv()
            left()
            x_step(2, 0)
            quad(0, first=True)
        for i in y_now[1:]:
            y_step(i)
        z_step(h, x_half)
        for dz in (h % z_chips, -h % z_chips) if not last else (h,):
            x_step(1, dz)
    for h in range(1, z_half):
        for dz in (h, z_chips - h):
            x_step(2, dz)
            quad(dz)
    x_step(2, z_half)
    quad(z_half)

    for c in range(bc):
        total = jnp.zeros((1, blk), f32)
        for r in range(br):
            block = acc[r * blk : (r + 1) * blk, c * blk : (c + 1) * blk] * op_ref[r, c].astype(f32)
            block = block * block
            acc[r * blk : (r + 1) * blk, c * blk : (c + 1) * blk] = block
            total += jnp.sum(block, axis=0, keepdims=True)
        totals[me, c : c + 1, :] = total
    far_first = sorted(
        ((dx, dz) for dx in range(X) for dz in range(z_chips) if dx or dz),
        key=lambda p: -(min(p[0], X - p[0]) + min(p[1], z_chips - p[1])),
    )
    for dx, dz in far_first:
        small(totals, me, {"gc": at(dx, dz)}, TOTALS).start()
    all_small(totals, gc - 1, {"gc": 0}, TOTALS).wait_recv()
    factor = float(gc * br * blk) / jnp.sum(totals[...], axis=0)
    for c in range(bc):
        o_ref[:, c * blk : (c + 1) * blk] = (acc[:, c * blk : (c + 1) * blk] * factor[c : c + 1, :]).astype(bf16)

    b_copy(0, (0, (gc - 1) * tile), 0, z_recv.at[0, 0, 0]).wait_send()
    a_copy(0, (0, (gr - 1) * tile), 0, y_recv.at[0, 0, 0]).wait_send()
    all_small(x_sums, X - 1, x_peers[0], X_SUMS).wait_send()
    all_small(z_sums, z_chips - 1, z_peers[0], Z_SUMS).wait_send()
    all_small(inverses, gr - 1, {"gr": 0}, INVERSES).wait_send()
    all_small(totals, gc - 1, {"gc": 0}, TOTALS).wait_send()


def solution(mesh):
    gc, gr = mesh.shape["gc"], mesh.shape["gr"]

    def shards(weights, in_pattern, out_pattern):
        rows, cols = weights.shape
        br, bc = in_pattern.shape
        blk = rows // br
        tile = CAP * blk + CODE
        z_chips, y_chips = gc // X, gr // CORES
        dma = pltpu.SemaphoreType.DMA
        bf16, f32 = jnp.bfloat16, jnp.float32
        return pl.pallas_call(
            functools.partial(kernel, gc, gr, blk),
            out_shape=jax.ShapeDtypeStruct(weights.shape, weights.dtype),
            in_specs=[pl.BlockSpec(memory_space=pl.ANY)] * 3,
            out_specs=pl.BlockSpec(memory_space=pltpu.VMEM),
            scratch_shapes=[
                pltpu.VMEM((rows, cols), bf16),
                pltpu.SMEM((br, bc), jnp.int32),
                pltpu.SMEM((br, bc), jnp.int32),
                pltpu.VMEM((gc * tile, blk), bf16),
                pltpu.VMEM((gr * tile, blk), bf16),
                pltpu.VMEM((z_chips, X * rows, cols), bf16),
                pltpu.VMEM((z_chips, rows, X * rows), bf16),
                pltpu.VMEM((rows, cols), f32),
                pltpu.VMEM((X, bc, blk), f32),
                pltpu.VMEM((z_chips, bc, blk), f32),
                pltpu.VMEM((gr, bc, blk), f32),
                pltpu.VMEM((gc, bc, blk), f32),
                dma((2, z_chips // 2, X + 1)),
                dma((2, X // 2, z_chips + 1)),
                dma((2, y_chips // 2, 2)),
                dma((y_chips,)),
                dma((4,)),
                dma((6,)),
                dma((3,)),
            ],
            compiler_params=pltpu.CompilerParams(
                collective_id=0, has_side_effects=True, vmem_limit_bytes=48 << 20
            ),
        )(weights, in_pattern, out_pattern)

    spec = P("gc", "gr")
    return jax.shard_map(shards, mesh=mesh, in_specs=(spec, spec, spec), out_specs=spec, check_vma=False)
```

time: 323 us -> 61.2 us (0.19)
  the two profiles are of different devices: /device:TPU:8 before, /device:TPU:1 now
where the time goes in v2:
time: 61.2 us; the launch traced here: 61 us
  Pallas kernels  58 us (95%)
  local copies, waits for them, and re-layouts  3.01 us (5%)
    pallas_call x1, Pallas kernels, shards(): pl.pallas_call(functools.partial(kernel, gc, gr, blk), out_shape=jax.Shap...  58 us
    unnamed x7, local copies, waits for them, and re-layouts  3.01 us

profile of v2, /device:TPU:1, one launch (start us, length us, event | category | flops | bytes accessed | tf_op | source)
XLA Modules:
  0.0 61.0 jit_solution(1058981118930457548)
XLA Ops:
  0.0 0.0 copy-start
  0.0 0.9 %copy-done = bf16[256,512]{1,0:T(8,128)(2,1)S(1)} copy-done((bf16[256,512]{1,0:T(8,128)(2,1)S(1)}, bf16[256,512]{1,0:T(8,128)(2,1)}, u32[]{:S(2)}) %copy-start) | copy-done | bytes 262168
  1.0 0.0 copy-start.1
  1.0 0.7 %copy-done.1 = s32[2,4]{1,0:T(2,128)S(1)} copy-done((s32[2,4]{1,0:T(2,128)S(1)}, s32[2,4]{1,0:T(2,128)}, u32[]{:S(2)}) %copy-start.1) | copy-done | bytes 56
  1.6 0.0 copy-start.2
  1.6 0.7 %copy-done.2 = s32[2,4]{1,0:T(2,128)S(1)} copy-done((s32[2,4]{1,0:T(2,128)S(1)}, s32[2,4]{1,0:T(2,128)}, u32[]{:S(2)}) %copy-start.2) | copy-done | bytes 56
  2.3 58.0 %shard_map.37 = bf16[256,512]{1,0:T(8,128)(2,1)S(1)} custom-call(bf16[256,512]{1,0:T(8,128)(2,1)S(1)} %copy-done, s32[2,4]{1,0:T(2,128)S(1)} %copy-done.1, s32[2,4]{1,0:T(2,128)S(1)} %copy-done.2), custom_call_target="tpu_custom_call" | custom-call | tf_op jit(solution)/shard_map/pallas_call | solution.py:331
  60.3 0.7 %copy.5 = bf16[256,512]{1,0:T(8,128)(2,1)} copy(bf16[256,512]{1,0:T(8,128)(2,1)S(1)} %shard_map.37) | data formatting | bytes 524288
Async XLA Ops:
  0.0 0.9 %copy-start = (bf16[256,512]{1,0:T(8,128)(2,1)S(1)}, bf16[256,512]{1,0:T(8,128)(2,1)}, u32[]{:S(2)}) copy-start(bf16[256,512]{1,0:T(8,128)(2,1)} %w_hbm.1) | copy-start | bytes 786436
  1.0 0.7 %copy-start.1 = (s32[2,4]{1,0:T(2,128)S(1)}, s32[2,4]{1,0:T(2,128)}, u32[]{:S(2)}) copy-start(s32[2,4]{1,0:T(2,128)} %ip_hbm.1) | copy-start | bytes 100
  1.6 0.7 %copy-start.2 = (s32[2,4]{1,0:T(2,128)S(1)}, s32[2,4]{1,0:T(2,128)}, u32[]{:S(2)}) copy-start(s32[2,4]{1,0:T(2,128)} %op_hbm.1) | copy-start | bytes 100

commit v3 on v2

--- a/solution.py
+++ b/solution.py
@@ -13,6 +13,116 @@
 CAP = 4
 CODE = 16
 P_ROWS = 208
+
+
+def halves(first, size):
+    low = (size // 2 + CODE - 1) // CODE * CODE
+    return (first, low), (first + low, size - low)
+
+
+def plan(z_chips, y_chips, tile):
+    row, hop, start, take = 5.5e-3, 1.75, 0.08, 0.05
+    spread, dot, left = 0.5, 0.4, 0.25
+    z_half, x_half, y_half = z_chips // 2, X // 2, y_chips // 2
+    Q, PX = X, z_chips
+    p_part, q_part = (0, P_ROWS), (P_ROWS, tile - P_ROWS)
+    now, serial, free, arrivals, steps, done = 0.0, 0, {}, [], [], set()
+    work = []
+
+    def part(kind, way, k, item):
+        if kind == "y":
+            return halves(0, tile)[item]
+        if kind == "z":
+            whole = q_part if item == Q else p_part
+            return halves(*whole)[way] if k == z_half else whole
+        whole = p_part if item == PX else q_part
+        return halves(*whole)[way] if k == x_half else whole
+
+    def arrive(when, step):
+        nonlocal serial
+        serial += 1
+        arrivals.append((when, serial, step))
+
+    def send(kind, way, k, item):
+        nonlocal now
+        now += start
+        free[kind, way] = max(now, free.get((kind, way), 0.0)) + part(kind, way, k, item)[1] * row
+        arrive(free[kind, way] + hop, (kind, way, k, item))
+
+    def small(kind, far, step):
+        arrive(max(now, free.get((kind, 0), 0.0), free.get((kind, 1), 0.0)) + hop + far, step)
+
+    def complete(dz):
+        if dz == 0:
+            need = {("x", d, k, PX) for d in range(2) for k in (1, 2)}
+        else:
+            ways = (0, 1) if dz == z_half else (1,) if dz < z_half else (0,)
+            need = {("z", s, min(dz, z_chips - dz), item) for s in ways for item in range(X + 1)}
+        need |= {("x", d, k, dz) for d in range(2) for k in range(1, x_half + 1)}
+        return need <= done
+
+    small("x", 1.0, ("x_sums",))
+    for s in range(2):
+        send("z", s, 1, Q)
+        send("x", s, 1, PX)
+    for piece in range(2):
+        for s in range(2):
+            send("y", s, 1, piece)
+    for s in range(2):
+        send("z", s, 1, 0)
+        send("x", s, 1, 0)
+    waiting = [dz for h in range(z_half + 1) for dz in dict.fromkeys((h, -h % z_chips))]
+    scaled = False
+    while arrivals or work:
+        arrivals.sort()
+        if not arrivals or (work and arrivals[0][0] > now):
+            step = work.pop(0)
+            steps.append(step)
+            now += {"spread": spread, "dot": dot, "left": left}[step[0]]
+            if step[0] == "spread":
+                done.add(step)
+        else:
+            when, _, step = arrivals.pop(0)
+            now = max(now, when) + take
+            steps.append(step)
+            done.add(step)
+            kind = step[0]
+            if kind == "z":
+                _, s, h, item = step
+                if h < z_half:
+                    send("z", s, h + 1, item)
+                if item == Q and (h < z_half or ("z", 1 - s, h, Q) in done):
+                    for d in range(2):
+                        send("x", d, 1, (h if s else -h) % z_chips)
+            elif kind == "x":
+                _, d, k, item = step
+                if k < x_half:
+                    send("x", d, k + 1, item)
+                if item == PX and (k < x_half or ("x", 1 - d, k, PX) in done):
+                    for s in range(2):
+                        send("z", s, 1, (k if d else -k) % X)
+            elif kind == "y":
+                _, s, h, piece = step
+                if h + 1 < y_half or (h < y_half and piece == s):
+                    send("y", s, h + 1, piece)
+            elif kind == "x_sums":
+                small("z", 4.0, ("z_sums",))
+            elif kind == "inverses":
+                work[:0] = [("left", zz) for zz in range(z_chips)]
+                scaled = True
+            if ("inverses",) not in done and not any(a[2][0] in ("y", "z_sums", "x_sums", "inverses") for a in arrivals):
+                steps.append(("share",))
+                small("y", 4.0, ("inverses",))
+        for dz in list(waiting):
+            if complete(dz):
+                waiting.remove(dz)
+                work.append(("spread", dz))
+        if scaled:
+            for dz in range(z_chips):
+                if ("spread", dz) in done and ("dot", dz) not in done:
+                    done.add(("dot", dz))
+                    work.append(("dot", dz))
+    return steps, now
 
 
 def kernel(
@@ -99,10 +209,6 @@
 
     pl.semaphore_wait(barrier, len(greeted))
 
-    def cut(first, size, which):
-        low = (size // 2 + CODE - 1) // CODE * CODE
-        return (first, low) if which == 0 else (first + low, size - low)
-
     P_PART, Q_PART = (0, P_ROWS), (P_ROWS, tile - P_ROWS)
 
     def b_copy(origin, part, dst, recv):
@@ -118,7 +224,7 @@
         sign = 1 - 2 * s
         part = Q_PART if item == Q else P_PART
         if h == z_half:
-            part = cut(*part, s)
+            part = halves(*part)[s]
         origin = at(0 if item == Q else item, -sign * (h - 1))
         return b_copy(origin, part, at(0, sign), z_recv.at[s, h - 1, item])
 
@@ -128,7 +234,7 @@
         sign = 1 - 2 * d
         part = P_PART if item == PX else Q_PART
         if k == x_half:
-            part = cut(*part, d)
+            part = halves(*part)[d]
         origin = at(-sign * (k - 1), 0 if item == PX else item)
         return b_copy(origin, part, at(sign, 0), x_recv.at[d, k - 1, item])
 
@@ -141,7 +247,7 @@
 
     def y_copy(s, h, piece):
         sign = 1 - 2 * s
-        return a_copy(at_y(-sign * (h - 1), core), cut(0, tile, piece), at_y(sign, core), y_recv.at[s, h - 1, piece])
+        return a_copy(at_y(-sign * (h - 1), core), halves(0, tile)[piece], at_y(sign, core), y_recv.at[s, h - 1, piece])
 
     def sib_copy(dy, c):
         return a_copy(at_y(dy, c), (0, tile), at_y(0, 1 - c), sib_recv.at[dy % y_chips])
@@ -160,28 +266,6 @@
         )
 
     X_SUMS, Z_SUMS, INVERSES, TOTALS = 2, 3, 4, 5
-
-    def y_step(h):
-        for piece in range(2):
-            for s in range(2):
-                if h < y_half or piece == s:
-                    y_copy(s, h, piece).wait_recv()
-                if h + 1 < y_half or (h < y_half and piece == s):
-                    y_copy(s, h + 1, piece).start()
-        for dy in (-h, h) if h < y_half else (h,):
-            sib_copy(dy, core).start()
-
-    def x_step(k, dz):
-        for d in range(2):
-            x_copy(d, k, dz).wait_recv()
-            if k < x_half:
-                x_copy(d, k + 1, dz).start()
-
-    def z_step(h, item):
-        for s in range(2):
-            z_copy(s, h, item).wait_recv()
-            if h < z_half:
-                z_copy(s, h + 1, item).start()
 
     def spread(t, buf, dst, r_base, c_base, inverse=None):
         codes = buf[pl.ds(rows(t, data), CODE), :].astype(f32)
@@ -199,24 +283,21 @@
             r, c = p // bc, p % bc
             dst[pl.ds(r_base + r * blk, blk), pl.ds(c_base + c * blk, blk)] = block
 
-    def left():
+    def z_row(dz):
+        return lax.rem(z + (dz + z_chips), z_chips)
+
+    def left(i):
         per = X * br // bc
-
-        @pl.loop(0, z_chips)
-        def _(zz):
-            for i in range(per):
-                t = zz * per + i
-                spread(t, abuf, adense.at[zz], 0, i * bc * blk, inverses[t])
-
-    def quad(dz, first=False):
-        zz = lax.rem(z + (dz + z_chips), z_chips)
+        for k in range(per):
+            t = i * per + k
+            spread(t, abuf, adense.at[i], 0, k * bc * blk, inverses[t])
+
+    def right(dz):
+        zz = z_row(dz)
 
         @pl.loop(0, X)
         def _(i):
             spread(zz * X + i, bbuf, bdense.at[zz], pl.multiple_of(i * (br * blk), blk), 0)
-
-        term = jnp.dot(adense[zz], bdense[zz], preferred_element_type=f32)
-        acc[...] = term if first else acc[...] + term
 
     for peer in x_peers:
         small(x_sums, x, peer, X_SUMS).start()
@@ -231,64 +312,59 @@
         x_copy(s, 1, 0).start()
     sib_copy(0, core).start()
 
-    all_small(x_sums, X - 1, x_peers[0], X_SUMS).wait_recv()
-    z_sums[z] = jnp.sum(x_sums[...], axis=0)
-    for peer in z_peers:
-        small(z_sums, z, peer, Z_SUMS).start()
-    for d in range(2):
-        x_copy(d, 1, PX).wait_recv()
-        x_copy(d, 2, PX).start()
-        for s in range(2):
-            z_copy(s, 1, (X - 1) if d == 0 else 1).start()
-    for d in range(2):
-        x_copy(d, 2, PX).wait_recv()
-    for s in range(2):
-        z_copy(s, 1, x_half).start()
-
-    for h in range(1, z_half + 1):
-        last = h == z_half
-        for s in range(2):
-            z_copy(s, h, Q).wait_recv()
-            if not last:
-                z_copy(s, h + 1, Q).start()
+    taken = set()
+    first = True
+    for step in plan(z_chips, y_chips, tile)[0]:
+        kind = step[0]
+        taken.add(step)
+        if kind == "z":
+            _, s, h, item = step
+            z_copy(s, h, item).wait_recv()
+            if h < z_half:
+                z_copy(s, h + 1, item).start()
+            if item == Q and (h < z_half or ("z", 1 - s, h, Q) in taken):
                 for d in range(2):
-                    x_copy(d, 1, (-h if s == 0 else h) % z_chips).start()
-        if last:
-            for d in range(2):
-                x_copy(d, 1, h).start()
-        if h == 1:
-            x_step(1, 0)
-        y_now = {1: (1,), 2: (2, 3)}.get(h, ())
-        z_step(h, 0)
-        if h == 1:
+                    x_copy(d, 1, (h if s else -h) % z_chips).start()
+        elif kind == "x":
+            _, d, k, item = step
+            x_copy(d, k, item).wait_recv()
+            if k < x_half:
+                x_copy(d, k + 1, item).start()
+            if item == PX and (k < x_half or ("x", 1 - d, k, PX) in taken):
+                for s in range(2):
+                    z_copy(s, 1, (k if d else -k) % X).start()
+        elif kind == "y":
+            _, s, h, piece = step
+            y_copy(s, h, piece).wait_recv()
+            if h + 1 < y_half or (h < y_half and piece == s):
+                y_copy(s, h + 1, piece).start()
+            other = ("y", s, h, 1 - piece) if h < y_half else ("y", 1 - s, h, 1 - piece)
+            if other in taken:
+                sib_copy(h if s or h == y_half else -h, core).start()
+        elif kind == "x_sums":
+            all_small(x_sums, X - 1, x_peers[0], X_SUMS).wait_recv()
+            z_sums[z] = jnp.sum(x_sums[...], axis=0)
+            for peer in z_peers:
+                small(z_sums, z, peer, Z_SUMS).start()
+        elif kind == "z_sums":
             all_small(z_sums, z_chips - 1, z_peers[0], Z_SUMS).wait_recv()
             inverses[mine] = 1.0 / jnp.sum(z_sums[...], axis=0)
-        for i in y_now[:1]:
-            y_step(i)
-        if h == 3:
-            y_step(4)
+        elif kind == "share":
             for dy in range(y_chips):
                 sib_copy(dy, 1 - core).wait_recv()
             for i in range(1, gr):
                 small(inverses, mine, {"gr": lax.rem(mine + i, gr)}, INVERSES).start()
-        z_step(h, 1)
-        z_step(h, X - 1)
-        if last:
+        elif kind == "inverses":
             all_small(inverses, gr - 1, {"gr": 0}, INVERSES).wait_recv()
-            left()
-            x_step(2, 0)
-            quad(0, first=True)
-        for i in y_now[1:]:
-            y_step(i)
-        z_step(h, x_half)
-        for dz in (h % z_chips, -h % z_chips) if not last else (h,):
-            x_step(1, dz)
-    for h in range(1, z_half):
-        for dz in (h, z_chips - h):
-            x_step(2, dz)
-            quad(dz)
-    x_step(2, z_half)
-    quad(z_half)
+        elif kind == "left":
+            left(step[1])
+        elif kind == "spread":
+            right(step[1])
+        elif kind == "dot":
+            zz = z_row(step[1])
+            term = jnp.dot(adense[zz], bdense[zz], preferred_element_type=f32)
+            acc[...] = term if first else acc[...] + term
+            first = False
 
     for c in range(bc):
         total = jnp.zeros((1, blk), f32)

time: 61.2 us -> 55.5 us (0.907)
  the two profiles are of different devices: /device:TPU:1 before, /device:TPU:24 now
where the time goes in v3:
time: 55.5 us; the launch traced here: 55.3 us
  Pallas kernels  52.3 us (94%)
  local copies, waits for them, and re-layouts  3.01 us (5%)
    pallas_call x1, Pallas kernels, shards(): pl.pallas_call(functools.partial(kernel, gc, gr, blk), out_shape=jax.Shap...  52.3 us
    unnamed x7, local copies, waits for them, and re-layouts  3.01 us

profile of v3, /device:TPU:24, one launch (start us, length us, event | category | flops | bytes accessed | tf_op | source)
XLA Modules:
  0.0 55.3 jit_solution(14831764033325403371)
XLA Ops:
  0.0 0.0 copy-start
  0.0 0.9 %copy-done = bf16[256,512]{1,0:T(8,128)(2,1)S(1)} copy-done((bf16[256,512]{1,0:T(8,128)(2,1)S(1)}, bf16[256,512]{1,0:T(8,128)(2,1)}, u32[]{:S(2)}) %copy-start) | copy-done | bytes 262168
  1.0 0.0 copy-start.1
  1.0 0.7 %copy-done.1 = s32[2,4]{1,0:T(2,128)S(1)} copy-done((s32[2,4]{1,0:T(2,128)S(1)}, s32[2,4]{1,0:T(2,128)}, u32[]{:S(2)}) %copy-start.1) | copy-done | bytes 56
  1.6 0.0 copy-start.2
  1.6 0.7 %copy-done.2 = s32[2,4]{1,0:T(2,128)S(1)} copy-done((s32[2,4]{1,0:T(2,128)S(1)}, s32[2,4]{1,0:T(2,128)}, u32[]{:S(2)}) %copy-start.2) | copy-done | bytes 56
  2.3 52.3 %shard_map.37 = bf16[256,512]{1,0:T(8,128)(2,1)S(1)} custom-call(bf16[256,512]{1,0:T(8,128)(2,1)S(1)} %copy-done, s32[2,4]{1,0:T(2,128)S(1)} %copy-done.1, s32[2,4]{1,0:T(2,128)S(1)} %copy-done.2), custom_call_target="tpu_custom_call" | custom-call | tf_op jit(solution)/shard_map/pallas_call | solution.py:407
  54.6 0.7 %copy.5 = bf16[256,512]{1,0:T(8,128)(2,1)} copy(bf16[256,512]{1,0:T(8,128)(2,1)S(1)} %shard_map.37) | data formatting | bytes 524288
Async XLA Ops:
  0.0 0.9 %copy-start = (bf16[256,512]{1,0:T(8,128)(2,1)S(1)}, bf16[256,512]{1,0:T(8,128)(2,1)}, u32[]{:S(2)}) copy-start(bf16[256,512]{1,0:T(8,128)(2,1)} %w_hbm.1) | copy-start | bytes 786436
  1.0 0.7 %copy-start.1 = (s32[2,4]{1,0:T(2,128)S(1)}, s32[2,4]{1,0:T(2,128)}, u32[]{:S(2)}) copy-start(s32[2,4]{1,0:T(2,128)} %ip_hbm.1) | copy-start | bytes 100
  1.6 0.7 %copy-start.2 = (s32[2,4]{1,0:T(2,128)S(1)}, s32[2,4]{1,0:T(2,128)}, u32[]{:S(2)}) copy-start(s32[2,4]{1,0:T(2,128)} %op_hbm.1) | copy-start | bytes 100

commit v4 on v3

v4 whole, which is shorter than its diff:
```python
import functools

import jax
import jax.numpy as jnp
from jax import lax
from jax.experimental import pallas as pl
from jax.experimental.pallas import tpu as pltpu
from jax.sharding import PartitionSpec as P

MESH = pl.DeviceIdType.MESH
X = 4
CORES = 2
CAP = 4
CODE = 16
P_ROWS = 208
ROW, HOP, START, TAKE = 5.5e-3, 1.75, 0.12, 0.08

FIRST = [("z", s, 1, X - 1) for s in range(2)] + [("x", d, 1, 4 + 1) for d in range(2)] + [("y", s, 1, 0) for s in range(2)]
FIRST += [("z", s, 1, 0) for s in range(2)] + [("x", d, 1, 0) for d in range(2)]


def follow(step, done, z_half, y_half):
    kind, way, k, item = step
    ways = range(2)
    both = (kind, 1 - way, k, item) in done
    last = {"x": X // 2, "y": y_half, "z": z_half}[kind]
    steps = [(kind, way, k + 1, item)] if k < last else []
    if kind == "z" and item == X - 1 and both:
        steps += [("x", d, 1, k) for d in ways]
    if kind == "x" and item == z_half + 1 and both:
        steps += [("z", s, 1, k) for s in ways]
    return steps


def halves(first, size):
    low = (size // 2 + CODE - 1) // CODE * CODE
    return (first, low), (first + low, size - low)


def plan(z_chips, y_chips, tile):
    row, hop, start, take = ROW, HOP, START, TAKE
    spread, dot, left = 0.5, 0.4, 0.25
    z_half, x_half, y_half = z_chips // 2, X // 2, y_chips // 2
    Q, PX = X - 1, z_half + 1
    now, serial, free, arrivals, steps, done = 0.0, 0, {}, [], [], set()
    work = []

    def size(kind, way, k, item):
        if kind == "y":
            return halves(0, tile)[way][1] if k == y_half else tile
        first = item != Q if kind == "z" else item == PX
        rows = P_ROWS if first else tile - P_ROWS
        if k == (z_half if kind == "z" else x_half):
            rows = halves(0, rows)[way][1]
        pair = item == 1 if kind == "z" else 0 < item < z_half
        return rows * (2 if pair else 1)

    def arrive(when, step):
        nonlocal serial
        serial += 1
        arrivals.append((when, serial, step))

    def send(kind, way, k, item):
        nonlocal now
        now += start
        free[kind, way] = max(now, free.get((kind, way), 0.0)) + size(kind, way, k, item) * row
        arrive(free[kind, way] + hop, (kind, way, k, item))

    def small(kind, far, step):
        arrive(max(now, free.get((kind, 0), 0.0), free.get((kind, 1), 0.0)) + hop + far, step)

    def complete(dz):
        h = min(dz, z_chips - dz)
        need = {("x", d, k, h) for d in range(2) for k in (1, 2)}
        if dz == 0:
            need |= {("x", d, k, PX) for d in range(2) for k in (1, 2)}
        else:
            ways = (0, 1) if dz == z_half else (1,) if dz < z_half else (0,)
            need |= {("z", s, h, item) for s in ways for item in range(X)}
        return need <= done

    small("x", 1.0, ("x_sums",))
    for step in FIRST:
        send(*step)
    waiting = [dz for h in range(z_half + 1) for dz in dict.fromkeys((h, -h % z_chips))]
    scaled = False
    while arrivals or work:
        arrivals.sort()
        if not arrivals or (work and arrivals[0][0] > now):
            step = work.pop(0)
            steps.append(step)
            now += {"spread": spread, "dot": dot, "left": left}[step[0]]
            if step[0] == "spread":
                done.add(step)
        else:
            when, _, step = arrivals.pop(0)
            now = max(now, when) + take
            steps.append(step)
            done.add(step)
            kind = step[0]
            if kind in ("x", "y", "z"):
                for following in follow(step, done, z_half, y_half):
                    send(*following)
            elif kind == "x_sums":
                small("z", 4.0, ("z_sums",))
            elif kind == "z_sums":
                small("y", 4.0, ("inverses",))
            if not scaled and not any(a[2][0] in ("y", "z_sums", "x_sums", "inverses") for a in arrivals):
                arrive(now + 2.0, ("all",))
                scaled = True
            if kind == "all":
                work[:0] = [("left", dy) for dy in range(y_chips)]
        for dz in list(waiting):
            if complete(dz):
                waiting.remove(dz)
                work.append(("spread", dz))
        if ("all",) in done:
            for dz in range(z_chips):
                if ("spread", dz) in done and ("dot", dz) not in done:
                    done.add(("dot", dz))
                    work.append(("dot", dz))
    return steps, now


def kernel(
    gc, gr, blk,
    w_hbm, ip_hbm, op_hbm, o_ref,
    w_ref, ip_ref, op_ref, pbuf, qbuf, abuf, bdense, adense, acc, x_sums, z_sums, inverses, totals,
    z_recv, x_recv, y_recv, sib_recv, small_recv, send_sem, local_sem,
):
    br, bc = ip_ref.shape
    z_chips, y_chips = gc // X, gr // CORES
    x_half, y_half, z_half = X // 2, y_chips // 2, z_chips // 2
    data = CAP * blk
    tile = data + CODE
    f32, bf16 = jnp.float32, jnp.bfloat16

    me = lax.axis_index("gc")
    mine = lax.axis_index("gr")
    x, z = lax.rem(me, X), lax.div(me, X)
    core, y = lax.rem(mine, CORES), lax.div(mine, CORES)

    def at(dx, dz):
        return lax.rem(z + (dz + z_chips), z_chips) * X + lax.rem(x + (dx + X), X)

    def at_y(dy, c):
        return lax.rem(y + (dy + y_chips), y_chips) * CORES + c

    def slot_of(d, n):
        d %= n
        return 2 * d - 1 if 0 < d <= n // 2 else 2 * (n - d) if d else 0

    loads = [
        pltpu.make_async_copy(src, dst, local_sem.at[i])
        for i, (src, dst) in enumerate(((ip_hbm, ip_ref), (w_hbm, w_ref), (op_hbm, op_ref)))
    ]
    for load in loads:
        load.start()
    barrier = pltpu.get_barrier_semaphore()
    x_peers = [{"gc": at(i, 0)} for i in range(1, X)]
    z_peers = [{"gc": at(0, i)} for i in range(1, z_chips)]
    y_peers = [{"gr": at_y(i, core)} for i in range(1, y_chips)]
    other_core = {"gr": at_y(0, 1 - core)}
    greeted = x_peers + z_peers + y_peers + [other_core]
    for peer in greeted:
        pl.semaphore_signal(barrier, inc=1, device_id=peer, device_id_type=MESH)
    for load in loads:
        load.wait()

    spots = br * bc
    on = [(ip_ref[p // bc, p % bc] > 0).astype(jnp.int32) for p in range(spots)]
    spare = CAP - sum(on)
    count = jnp.int32(0)
    place = [jnp.int32(0)] * CAP
    for p in range(spots):
        filler = jnp.logical_and(on[p] == 0, spare > 0).astype(jnp.int32)
        spare = spare - filler
        used = on[p] + filler
        for s in range(CAP):
            place[s] = place[s] + jnp.where(count == s, used, 0) * p
        count = count + used

    def reach(p):
        return range(max(0, p - (spots - CAP)), min(CAP - 1, p) + 1)

    def block_of(p):
        r, c = p // bc, p % bc
        return w_ref[r * blk : (r + 1) * blk, c * blk : (c + 1) * blk]

    for c in range(bc):
        total = jnp.zeros((1, blk), f32)
        for r in range(br):
            block = block_of(r * bc + c).astype(f32)
            total += jnp.sum(block, axis=0, keepdims=True) * on[r * bc + c].astype(f32)
        x_sums[0, c : c + 1, :] = total
    def put(first, block):
        size = block.shape[0]
        abuf[0, first : first + size, :] = block
        cut = min(max(P_ROWS - first, 0), size)
        if cut > 0:
            pbuf[0, first : first + cut, :] = block[:cut]
        if cut < size:
            qbuf[0, first + cut - P_ROWS : first + size - P_ROWS, :] = block[cut:]

    code_row = lax.broadcasted_iota(jnp.int32, (CODE, blk), 0)
    codes = jnp.zeros((CODE, blk), f32)
    for s in range(CAP):
        slot = sum(
            block_of(p) * jnp.full((1, blk), jnp.where(place[s] == p, on[p], 0).astype(f32)).astype(bf16)
            for p in range(s, s + spots - CAP + 1)
        )
        put(s * blk, slot)
        codes = jnp.where(code_row == s, place[s].astype(f32), codes)
    put(data, codes.astype(bf16))

    pl.semaphore_wait(barrier, len(greeted))

    down = {"z": [{"gc": at(0, 1)}, {"gc": at(0, -1)}], "x": [{"gc": at(1, 0)}, {"gc": at(-1, 0)}],
            "y": [{"gr": at_y(1, core)}, {"gr": at_y(-1, core)}]}
    landed = {"z": z_recv, "x": x_recv, "y": y_recv}
    sent = {"p": send_sem.at[0], "q": send_sem.at[7], "a": send_sem.at[1]}
    which = {"p": pbuf, "q": qbuf, "a": abuf}

    def move(name, src, dst, count, rows, sem, peer):
        ref, (first, size) = which[name], rows
        return pltpu.make_async_remote_copy(
            src_ref=ref.at[src : src + count, first : first + size, :],
            dst_ref=ref.at[dst : dst + count, first : first + size, :],
            send_sem=sent[name], recv_sem=sem, device_id=peer, device_id_type=MESH,
        )

    def link(kind, way, k, item):
        sign = 1 - 2 * way
        n = {"z": z_chips, "x": X, "y": y_chips}[kind]
        here, there = slot_of(-sign * (k - 1), n), slot_of(-sign * k, n)
        whole = {"p": (0, P_ROWS), "q": (0, tile - P_ROWS), "a": (0, tile)}
        count = 1
        if kind == "y":
            name, src, dst = "a", here, there
        elif (kind == "z") == (item == (X - 1 if kind == "z" else z_half + 1)):
            name = "q"
            if kind == "z":
                src, dst = here, there
            else:
                z0 = 2 * item - 1 if item else 0
                count = 2 if 0 < item < z_half else 1
                src, dst = here * z_chips + z0, there * z_chips + z0
        else:
            name = "p"
            if kind == "x":
                src, dst = here, there
            else:
                x0 = 2 * item - 1 if item else 0
                count = 2 if item == 1 else 1
                src, dst = here * X + x0, there * X + x0
        rows = halves(*whole[name])[way] if k == n // 2 else whole[name]
        sem = landed[kind].at[way, k - 1] if kind == "y" else landed[kind].at[way, k - 1, item]
        return move(name, src, dst, count, rows, sem, down[kind][way])

    def sib_copy(dy):
        i = slot_of(dy, y_chips)
        return move("a", i, y_chips + i, 1, (0, tile), sib_recv.at[i], other_core)

    def small(ref, index, peer, k):
        return pltpu.make_async_remote_copy(
            src_ref=ref.at[0], dst_ref=ref.at[index], send_sem=send_sem.at[k], recv_sem=small_recv.at[k - 2],
            device_id=peer, device_id_type=MESH,
        )

    def all_small(ref, n, peer, k):
        view = ref.at[pl.ds(0, n)]
        return pltpu.make_async_remote_copy(
            src_ref=view, dst_ref=view, send_sem=send_sem.at[k], recv_sem=small_recv.at[k - 2],
            device_id=peer, device_id_type=MESH,
        )

    X_SUMS, Z_SUMS, INVERSES, TOTALS, PASSED = 2, 3, 4, 5, 6

    def pass_on():
        return pltpu.make_async_remote_copy(
            src_ref=inverses.at[pl.ds(0, y_chips)], dst_ref=inverses.at[pl.ds(y_chips, y_chips)],
            send_sem=send_sem.at[PASSED], recv_sem=small_recv.at[PASSED - 2],
            device_id=other_core, device_id_type=MESH,
        )

    def spread(load, dst, r_base, c_base, inverse=None):
        codes = load(data, CODE).astype(f32)
        places = [codes[s : s + 1, :] for s in range(CAP)]
        slots = [load(s * blk, blk) for s in range(CAP)]
        if inverse is not None:
            for s in range(CAP):
                factor = sum(
                    inverse[c : c + 1, :] * sum((places[s] == float(r * bc + c)).astype(f32) for r in range(br))
                    for c in range(bc)
                )
                slots[s] = (slots[s].astype(f32) * factor).astype(bf16)
        for p in range(spots):
            block = sum(slots[s] * (places[s] == float(p)).astype(f32).astype(bf16) for s in reach(p))
            r, c = p // bc, p % bc
            dst[pl.ds(r_base + r * blk, blk), pl.ds(c_base + c * blk, blk)] = block

    def left(dy):
        zz = lax.rem(y + dy, y_chips)
        for other in range(CORES):
            i = other * y_chips + slot_of(dy, y_chips)
            c_base = pl.multiple_of((core if other == 0 else 1 - core) * (bc * blk), blk)
            spread(lambda first, size, i=i: abuf[i, first : first + size, :], adense.at[zz], 0, c_base, inverses[i])

    def right(dz):
        zs = slot_of(dz, z_chips)

        @pl.loop(0, X)
        def _(i):
            def load(first, size):
                cut = min(max(P_ROWS - first, 0), size)
                parts = []
                if cut > 0:
                    parts.append(pbuf[zs * X + i, first : first + cut, :])
                if cut < size:
                    parts.append(qbuf[i * z_chips + zs, first + cut - P_ROWS : first + size - P_ROWS, :])
                return parts[0] if len(parts) == 1 else jnp.concatenate(parts, axis=0)

            dx = i + jnp.where(i == 2, 1, 0) - jnp.where(i == 3, 1, 0)
            spread(load, bdense.at[zs], pl.multiple_of(lax.rem(x + dx, X) * (br * blk), blk), 0)

    for i, peer in enumerate(x_peers):
        small(x_sums, X - 1 - i, peer, X_SUMS).start()
    for step in FIRST:
        link(*step).start()
    sib_copy(0).start()

    taken = set()
    first = True
    for step in plan(z_chips, y_chips, tile)[0]:
        kind = step[0]
        if kind in landed:
            link(*step).wait_recv()
            for following in follow(step, taken, z_half, y_half):
                link(*following).start()
            if kind == "y" and (step[2] < y_half or ("y", 1 - step[1], y_half, 0) in taken):
                sib_copy(step[2] if step[1] else -step[2]).start()
        elif kind == "x_sums":
            all_small(x_sums, X - 1, x_peers[0], X_SUMS).wait_recv()
            z_sums[0] = jnp.sum(x_sums[...], axis=0)
            for i, peer in enumerate(z_peers):
                small(z_sums, z_chips - 1 - i, peer, Z_SUMS).start()
        elif kind == "z_sums":
            all_small(z_sums, z_chips - 1, z_peers[0], Z_SUMS).wait_recv()
            inverses[0] = 1.0 / jnp.sum(z_sums[...], axis=0)
            for i, peer in enumerate(y_peers):
                small(inverses, slot_of(-1 - i, y_chips), peer, INVERSES).start()
        elif kind == "inverses":
            all_small(inverses, y_chips - 1, y_peers[0], INVERSES).wait_recv()
            pass_on().start()
        elif kind == "all":
            for dy in range(y_chips):
                sib_copy(dy).wait_recv()
            pass_on().wait_recv()
        elif kind == "left":
            left(step[1])
        elif kind == "spread":
            right(step[1])
        elif kind == "dot":
            zz = lax.rem(z + step[1], z_chips)
            term = jnp.dot(adense[zz], bdense[slot_of(step[1], z_chips)], preferred_element_type=f32)
            acc[...] = term if first else acc[...] + term
            first = False
        taken.add(step)

    for c in range(bc):
        total = jnp.zeros((1, blk), f32)
        for r in range(br):
            block = acc[r * blk : (r + 1) * blk, c * blk : (c + 1) * blk] * op_ref[r, c].astype(f32)
            block = block * block
            acc[r * blk : (r + 1) * blk, c * blk : (c + 1) * blk] = block
            total += jnp.sum(block, axis=0, keepdims=True)
        totals[0, c : c + 1, :] = total
    far_first = sorted(
        ((dx, dz) for dx in range(X) for dz in range(z_chips) if dx or dz),
        key=lambda p: -(min(p[0], X - p[0]) + min(p[1], z_chips - p[1])),
    )
    for dx, dz in far_first:
        small(totals, -dz % z_chips * X + -dx % X, {"gc": at(dx, dz)}, TOTALS).start()
    all_small(totals, gc - 1, {"gc": 0}, TOTALS).wait_recv()
    factor = float(gc * br * blk) / jnp.sum(totals[...], axis=0)
    for c in range(bc):
        o_ref[:, c * blk : (c + 1) * blk] = (acc[:, c * blk : (c + 1) * blk] * factor[c : c + 1, :]).astype(bf16)

    neighbour = down["x"][0]
    move("p", 0, 0, gc - 1, (0, P_ROWS), x_recv.at[0, 0, 0], neighbour).wait_send()
    move("q", 0, 0, gc - 1, (0, tile - P_ROWS), x_recv.at[0, 0, 0], neighbour).wait_send()
    move("a", 0, 0, gr - 1, (0, tile), sib_recv.at[0], other_core).wait_send()
    all_small(x_sums, X - 1, x_peers[0], X_SUMS).wait_send()
    all_small(z_sums, z_chips - 1, z_peers[0], Z_SUMS).wait_send()
    all_small(inverses, y_chips - 1, y_peers[0], INVERSES).wait_send()
    pass_on().wait_send()
    all_small(totals, gc - 1, {"gc": 0}, TOTALS).wait_send()


def solution(mesh):
    gc, gr = mesh.shape["gc"], mesh.shape["gr"]

    def shards(weights, in_pattern, out_pattern):
        rows, cols = weights.shape
        br, bc = in_pattern.shape
        blk = rows // br
        tile = CAP * blk + CODE
        z_chips, y_chips = gc // X, gr // CORES
        dma = pltpu.SemaphoreType.DMA
        bf16, f32 = jnp.bfloat16, jnp.float32
        return pl.pallas_call(
            functools.partial(kernel, gc, gr, blk),
            out_shape=jax.ShapeDtypeStruct(weights.shape, weights.dtype),
            in_specs=[pl.BlockSpec(memory_space=pl.ANY)] * 3,
            out_specs=pl.BlockSpec(memory_space=pltpu.VMEM),
            scratch_shapes=[
                pltpu.VMEM((rows, cols), bf16),
                pltpu.SMEM((br, bc), jnp.int32),
                pltpu.SMEM((br, bc), jnp.int32),
                pltpu.VMEM((gc, P_ROWS, blk), bf16),
                pltpu.VMEM((gc, tile - P_ROWS, blk), bf16),
                pltpu.VMEM((gr, tile, blk), bf16),
                pltpu.VMEM((z_chips, X * rows, cols), bf16),
                pltpu.VMEM((z_chips, rows, X * rows), bf16),
                pltpu.VMEM((rows, cols), f32),
                pltpu.VMEM((X, bc, blk), f32),
                pltpu.VMEM((z_chips, bc, blk), f32),
                pltpu.VMEM((gr, bc, blk), f32),
                pltpu.VMEM((gc, bc, blk), f32),
                dma((2, z_chips // 2, X)),
                dma((2, X // 2, z_chips // 2 + 2)),
                dma((2, y_chips // 2)),
                dma((y_chips,)),
                dma((5,)),
                dma((8,)),
                dma((3,)),
            ],
            compiler_params=pltpu.CompilerParams(
                collective_id=0, has_side_effects=True, vmem_limit_bytes=48 << 20
            ),
        )(weights, in_pattern, out_pattern)

    spec = P("gc", "gr")
    return jax.shard_map(shards, mesh=mesh, in_specs=(spec, spec, spec), out_specs=spec, check_vma=False)
```

time: 55.5 us -> 56.3 us (1.014)
  the two profiles are of different devices: /device:TPU:24 before, /device:TPU:2 now
where the time goes in v4:
time: 56.3 us; the launch traced here: 56.1 us
  Pallas kernels  53.1 us (94%)
  local copies, waits for them, and re-layouts  3.01 us (5%)
    pallas_call x1, Pallas kernels, shards(): pl.pallas_call(functools.partial(kernel, gc, gr, blk), out_shape=jax.Shap...  53.1 us
    unnamed x7, local copies, waits for them, and re-layouts  3.01 us

profile of v4, /device:TPU:2, one launch (start us, length us, event | category | flops | bytes accessed | tf_op | source)
XLA Modules:
  0.0 56.1 jit_solution(740700077655080878)
XLA Ops:
  0.0 0.0 copy-start
  0.0 0.9 %copy-done = bf16[256,512]{1,0:T(8,128)(2,1)S(1)} copy-done((bf16[256,512]{1,0:T(8,128)(2,1)S(1)}, bf16[256,512]{1,0:T(8,128)(2,1)}, u32[]{:S(2)}) %copy-start) | copy-done | bytes 262168
  1.0 0.0 copy-start.1
  1.0 0.7 %copy-done.1 = s32[2,4]{1,0:T(2,128)S(1)} copy-done((s32[2,4]{1,0:T(2,128)S(1)}, s32[2,4]{1,0:T(2,128)}, u32[]{:S(2)}) %copy-start.1) | copy-done | bytes 56
  1.6 0.0 copy-start.2
  1.6 0.7 %copy-done.2 = s32[2,4]{1,0:T(2,128)S(1)} copy-done((s32[2,4]{1,0:T(2,128)S(1)}, s32[2,4]{1,0:T(2,128)}, u32[]{:S(2)}) %copy-start.2) | copy-done | bytes 56
  2.3 53.1 %shard_map.37 = bf16[256,512]{1,0:T(8,128)(2,1)S(1)} custom-call(bf16[256,512]{1,0:T(8,128)(2,1)S(1)} %copy-done, s32[2,4]{1,0:T(2,128)S(1)} %copy-done.1, s32[2,4]{1,0:T(2,128)S(1)} %copy-done.2), custom_call_target="tpu_custom_call" | custom-call | tf_op jit(solution)/shard_map/pallas_call | solution.py:411
  55.4 0.7 %copy.5 = bf16[256,512]{1,0:T(8,128)(2,1)} copy(bf16[256,512]{1,0:T(8,128)(2,1)S(1)} %shard_map.37) | data formatting | bytes 524288
Async XLA Ops:
  0.0 0.9 %copy-start = (bf16[256,512]{1,0:T(8,128)(2,1)S(1)}, bf16[256,512]{1,0:T(8,128)(2,1)}, u32[]{:S(2)}) copy-start(bf16[256,512]{1,0:T(8,128)(2,1)} %w_hbm.1) | copy-start | bytes 786436
  1.0 0.7 %copy-start.1 = (s32[2,4]{1,0:T(2,128)S(1)}, s32[2,4]{1,0:T(2,128)}, u32[]{:S(2)}) copy-start(s32[2,4]{1,0:T(2,128)} %ip_hbm.1) | copy-start | bytes 100
  1.6 0.7 %copy-start.2 = (s32[2,4]{1,0:T(2,128)S(1)}, s32[2,4]{1,0:T(2,128)}, u32[]{:S(2)}) copy-start(s32[2,4]{1,0:T(2,128)} %op_hbm.1) | copy-start | bytes 100

commit v5 on v4

--- a/solution.py
+++ b/solution.py
@@ -12,23 +12,50 @@
 CORES = 2
 CAP = 4
 CODE = 16
-P_ROWS = 208
-ROW, HOP, START, TAKE = 5.5e-3, 1.75, 0.12, 0.08
-
-FIRST = [("z", s, 1, X - 1) for s in range(2)] + [("x", d, 1, 4 + 1) for d in range(2)] + [("y", s, 1, 0) for s in range(2)]
-FIRST += [("z", s, 1, 0) for s in range(2)] + [("x", d, 1, 0) for d in range(2)]
-
-
-def follow(step, done, z_half, y_half):
-    kind, way, k, item = step
+P_ROWS = 192
+ROW, HOP, START, TAKE = 5.5e-3, 2.4, 0.08, 0.05
+
+ALL = 2
+RELAYS = 3
+P_PIECES, Q_PIECES, Y_PIECES = (ALL,), (0, 1), (0, 1)
+
+
+def slot_of(d, n):
+    d %= n
+    return 2 * d - 1 if 0 < d <= n // 2 else 2 * (n - d) if d else 0
+
+
+def pieces(kind, item, z_chips):
+    if kind == "y":
+        return Y_PIECES
+    return Q_PIECES if (kind == "z") == (item == (X if kind == "z" else z_chips)) else P_PIECES
+
+
+def ring(kind, z_chips, y_chips):
+    return {"x": X, "y": y_chips, "z": z_chips}[kind]
+
+
+def goes(way, k, piece, n):
+    return k < n // 2 or piece in (ALL, way)
+
+
+def first_copies(z_chips):
     ways = range(2)
-    both = (kind, 1 - way, k, item) in done
-    last = {"x": X // 2, "y": y_half, "z": z_half}[kind]
-    steps = [(kind, way, k + 1, item)] if k < last else []
-    if kind == "z" and item == X - 1 and both:
-        steps += [("x", d, 1, k) for d in ways]
-    if kind == "x" and item == z_half + 1 and both:
-        steps += [("z", s, 1, k) for s in ways]
+    order = (("z", X), ("x", z_chips), ("y", 0), ("z", 0), ("x", 0))
+    return [(kind, way, 1, item, piece) for kind, item in order for piece in pieces(kind, item, z_chips) for way in ways]
+
+
+def follow(step, done, z_chips, y_chips):
+    kind, way, k, item, piece = step
+    ways = range(2)
+    n = ring(kind, z_chips, y_chips)
+    steps = [(kind, way, k + 1, item, piece)] if k < n // 2 and goes(way, k + 1, piece, n) else []
+    whole = k < n // 2 or piece != ALL or (kind, 1 - way, k, item, piece) in done
+    came = slot_of(k if way else -k, n)
+    if kind == "z" and item == X and whole:
+        steps += [("x", d, 1, came, piece) for d in ways]
+    if kind == "x" and item == z_chips and whole:
+        steps += [("z", s, 1, came, piece) for s in ways]
     return steps
 
 
@@ -41,46 +68,49 @@
     row, hop, start, take = ROW, HOP, START, TAKE
     spread, dot, left = 0.5, 0.4, 0.25
     z_half, x_half, y_half = z_chips // 2, X // 2, y_chips // 2
-    Q, PX = X - 1, z_half + 1
+    Q, PX = X, z_chips
     now, serial, free, arrivals, steps, done = 0.0, 0, {}, [], [], set()
     work = []
 
-    def size(kind, way, k, item):
-        if kind == "y":
-            return halves(0, tile)[way][1] if k == y_half else tile
+    def size(kind, way, k, item, piece):
         first = item != Q if kind == "z" else item == PX
-        rows = P_ROWS if first else tile - P_ROWS
-        if k == (z_half if kind == "z" else x_half):
-            rows = halves(0, rows)[way][1]
-        pair = item == 1 if kind == "z" else 0 < item < z_half
-        return rows * (2 if pair else 1)
+        rows = tile if kind == "y" else P_ROWS if first else tile - P_ROWS
+        if piece != ALL:
+            return halves(0, rows)[piece][1]
+        return halves(0, rows)[way][1] if k == ring(kind, z_chips, y_chips) // 2 else rows
 
     def arrive(when, step):
         nonlocal serial
         serial += 1
         arrivals.append((when, serial, step))
 
-    def send(kind, way, k, item):
+    def send(*step):
         nonlocal now
         now += start
-        free[kind, way] = max(now, free.get((kind, way), 0.0)) + size(kind, way, k, item) * row
-        arrive(free[kind, way] + hop, (kind, way, k, item))
+        free[step[:2]] = max(now, free.get(step[:2], 0.0)) + size(*step) * row
+        arrive(free[step[:2]] + hop, step)
 
     def small(kind, far, step):
         arrive(max(now, free.get((kind, 0), 0.0), free.get((kind, 1), 0.0)) + hop + far, step)
 
     def complete(dz):
         h = min(dz, z_chips - dz)
-        need = {("x", d, k, h) for d in range(2) for k in (1, 2)}
+        parts = [("x", d, k, slot_of(dz, z_chips)) for d in range(2) for k in (1, 2)]
         if dz == 0:
-            need |= {("x", d, k, PX) for d in range(2) for k in (1, 2)}
+            parts += [("x", d, k, PX) for d in range(2) for k in (1, 2)]
         else:
             ways = (0, 1) if dz == z_half else (1,) if dz < z_half else (0,)
-            need |= {("z", s, h, item) for s in ways for item in range(X)}
+            parts += [("z", s, h, item) for s in ways for item in range(X + 1)]
+        need = {
+            (kind, way, k, item, piece)
+            for kind, way, k, item in parts
+            for piece in pieces(kind, item, z_chips)
+            if goes(way, k, piece, ring(kind, z_chips, y_chips))
+        }
         return need <= done
 
-    small("x", 1.0, ("x_sums",))
-    for step in FIRST:
+    arrive(2.2, ("ready", 0))
+    for step in first_copies(z_chips):
         send(*step)
     waiting = [dz for h in range(z_half + 1) for dz in dict.fromkeys((h, -h % z_chips))]
     scaled = False
@@ -99,13 +129,19 @@
             done.add(step)
             kind = step[0]
             if kind in ("x", "y", "z"):
-                for following in follow(step, done, z_half, y_half):
+                for following in follow(step, done, z_chips, y_chips):
                     send(*following)
-            elif kind == "x_sums":
-                small("z", 4.0, ("z_sums",))
+            elif kind == "ready":
+                if step[1] + 1 < RELAYS:
+                    arrive(now + 2.2, ("ready", step[1] + 1))
+                if step[1] == 0:
+                    small("x", 1.0, ("x_sums",))
             elif kind == "z_sums":
                 small("y", 4.0, ("inverses",))
-            if not scaled and not any(a[2][0] in ("y", "z_sums", "x_sums", "inverses") for a in arrivals):
+            if step in (("x_sums",), ("ready", RELAYS - 1)) and {("x_sums",), ("ready", RELAYS - 1)} <= done:
+                steps.append(("column",))
+                small("z", 4.0, ("z_sums",))
+            if not scaled and not any(a[2][0] in ("y", "z_sums", "x_sums", "ready", "inverses") for a in arrivals):
                 arrive(now + 2.0, ("all",))
                 scaled = True
             if kind == "all":
@@ -126,7 +162,7 @@
     gc, gr, blk,
     w_hbm, ip_hbm, op_hbm, o_ref,
     w_ref, ip_ref, op_ref, pbuf, qbuf, abuf, bdense, adense, acc, x_sums, z_sums, inverses, totals,
-    z_recv, x_recv, y_recv, sib_recv, small_recv, send_sem, local_sem,
+    z_recv, x_recv, y_recv, sib_recv, small_recv, send_sem, local_sem, ready_sem,
 ):
     br, bc = ip_ref.shape
     z_chips, y_chips = gc // X, gr // CORES
@@ -145,10 +181,6 @@
 
     def at_y(dy, c):
         return lax.rem(y + (dy + y_chips), y_chips) * CORES + c
-
-    def slot_of(d, n):
-        d %= n
-        return 2 * d - 1 if 0 < d <= n // 2 else 2 * (n - d) if d else 0
 
     loads = [
         pltpu.make_async_copy(src, dst, local_sem.at[i])
@@ -161,7 +193,8 @@
     z_peers = [{"gc": at(0, i)} for i in range(1, z_chips)]
     y_peers = [{"gr": at_y(i, core)} for i in range(1, y_chips)]
     other_core = {"gr": at_y(0, 1 - core)}
-    greeted = x_peers + z_peers + y_peers + [other_core]
+    nearest = [{"gc": at(1, 0)}, {"gc": at(-1, 0)}, {"gc": at(0, 1)}, {"gc": at(0, -1)}, {"gr": at_y(1, core)}, {"gr": at_y(-1, core)}]
+    greeted = nearest + [other_core]
     for peer in greeted:
         pl.semaphore_signal(barrier, inc=1, device_id=peer, device_id_type=MESH)
     for load in loads:
@@ -229,33 +262,24 @@
             send_sem=sent[name], recv_sem=sem, device_id=peer, device_id_type=MESH,
         )
 
-    def link(kind, way, k, item):
+    def link(kind, way, k, item, piece):
         sign = 1 - 2 * way
-        n = {"z": z_chips, "x": X, "y": y_chips}[kind]
+        n = ring(kind, z_chips, y_chips)
         here, there = slot_of(-sign * (k - 1), n), slot_of(-sign * k, n)
         whole = {"p": (0, P_ROWS), "q": (0, tile - P_ROWS), "a": (0, tile)}
-        count = 1
         if kind == "y":
             name, src, dst = "a", here, there
-        elif (kind == "z") == (item == (X - 1 if kind == "z" else z_half + 1)):
-            name = "q"
-            if kind == "z":
-                src, dst = here, there
-            else:
-                z0 = 2 * item - 1 if item else 0
-                count = 2 if 0 < item < z_half else 1
-                src, dst = here * z_chips + z0, there * z_chips + z0
+        elif kind == "z":
+            name = "q" if item == X else "p"
+            src, dst = (here, there) if item == X else (here * X + item, there * X + item)
         else:
-            name = "p"
-            if kind == "x":
-                src, dst = here, there
-            else:
-                x0 = 2 * item - 1 if item else 0
-                count = 2 if item == 1 else 1
-                src, dst = here * X + x0, there * X + x0
-        rows = halves(*whole[name])[way] if k == n // 2 else whole[name]
-        sem = landed[kind].at[way, k - 1] if kind == "y" else landed[kind].at[way, k - 1, item]
-        return move(name, src, dst, count, rows, sem, down[kind][way])
+            name = "p" if item == z_chips else "q"
+            src, dst = (here, there) if item == z_chips else (here * z_chips + item, there * z_chips + item)
+        rows = whole[name]
+        if piece != ALL or k == n // 2:
+            rows = halves(*rows)[way if piece == ALL else piece]
+        sem = landed[kind].at[way, k - 1, 2 * item + piece % 2]
+        return move(name, src, dst, 1, rows, sem, down[kind][way])
 
     def sib_copy(dy):
         i = slot_of(dy, y_chips)
@@ -323,9 +347,12 @@
             dx = i + jnp.where(i == 2, 1, 0) - jnp.where(i == 3, 1, 0)
             spread(load, bdense.at[zs], pl.multiple_of(lax.rem(x + dx, X) * (br * blk), blk), 0)
 
-    for i, peer in enumerate(x_peers):
-        small(x_sums, X - 1 - i, peer, X_SUMS).start()
-    for step in FIRST:
+    def relay(i):
+        for peer in nearest:
+            pl.semaphore_signal(ready_sem.at[i], inc=1, device_id=peer, device_id_type=MESH)
+
+    relay(0)
+    for step in first_copies(z_chips):
         link(*step).start()
     sib_copy(0).start()
 
@@ -335,13 +362,23 @@
         kind = step[0]
         if kind in landed:
             link(*step).wait_recv()
-            for following in follow(step, taken, z_half, y_half):
+            for following in follow(step, taken, z_chips, y_chips):
                 link(*following).start()
-            if kind == "y" and (step[2] < y_half or ("y", 1 - step[1], y_half, 0) in taken):
-                sib_copy(step[2] if step[1] else -step[2]).start()
+            if kind == "y":
+                _, way, k, _, piece = step
+                if ("y", way if k < y_half else 1 - way, k, 0, 1 - piece) in taken:
+                    sib_copy(k if way else -k).start()
+        elif kind == "ready":
+            pl.semaphore_wait(ready_sem.at[step[1]], len(nearest))
+            if step[1] + 1 < RELAYS:
+                relay(step[1] + 1)
+            if step[1] == 0:
+                for i, peer in enumerate(x_peers):
+                    small(x_sums, X - 1 - i, peer, X_SUMS).start()
         elif kind == "x_sums":
             all_small(x_sums, X - 1, x_peers[0], X_SUMS).wait_recv()
             z_sums[0] = jnp.sum(x_sums[...], axis=0)
+        elif kind == "column":
             for i, peer in enumerate(z_peers):
                 small(z_sums, z_chips - 1 - i, peer, Z_SUMS).start()
         elif kind == "z_sums":
@@ -427,13 +464,14 @@
                 pltpu.VMEM((z_chips, bc, blk), f32),
                 pltpu.VMEM((gr, bc, blk), f32),
                 pltpu.VMEM((gc, bc, blk), f32),
-                dma((2, z_chips // 2, X)),
-                dma((2, X // 2, z_chips // 2 + 2)),
-                dma((2, y_chips // 2)),
+                dma((2, z_chips // 2, 2 * (X + 1))),
+                dma((2, X // 2, 2 * (z_chips + 1))),
+                dma((2, y_chips // 2, 2)),
                 dma((y_chips,)),
                 dma((5,)),
                 dma((8,)),
                 dma((3,)),
+                pltpu.SemaphoreType.REGULAR((RELAYS,)),
             ],
             compiler_params=pltpu.CompilerParams(
                 collective_id=0, has_side_effects=True, vmem_limit_bytes=48 << 20

time: 56.3 us -> 53.6 us (0.952)
  the two profiles are of different devices: /device:TPU:2 before, /device:TPU:24 now
where the time goes in v5:
time: 53.6 us; the launch traced here: 53.4 us
  Pallas kernels  50.4 us (94%)
  local copies, waits for them, and re-layouts  3.01 us (6%)
    pallas_call x1, Pallas kernels, shards(): pl.pallas_call(functools.partial(kernel, gc, gr, blk), out_shape=jax.Shap...  50.4 us
    unnamed x7, local copies, waits for them, and re-layouts  3.01 us

profile of v5, /device:TPU:24, one launch (start us, length us, event | category | flops | bytes accessed | tf_op | source)
XLA Modules:
  0.0 53.4 jit_solution(13137637667557666347)
XLA Ops:
  0.0 0.0 copy-start
  0.0 0.9 %copy-done = bf16[256,512]{1,0:T(8,128)(2,1)S(1)} copy-done((bf16[256,512]{1,0:T(8,128)(2,1)S(1)}, bf16[256,512]{1,0:T(8,128)(2,1)}, u32[]{:S(2)}) %copy-start) | copy-done | bytes 262168
  1.0 0.0 copy-start.1
  1.0 0.7 %copy-done.1 = s32[2,4]{1,0:T(2,128)S(1)} copy-done((s32[2,4]{1,0:T(2,128)S(1)}, s32[2,4]{1,0:T(2,128)}, u32[]{:S(2)}) %copy-start.1) | copy-done | bytes 56
  1.6 0.0 copy-start.2
  1.6 0.7 %copy-done.2 = s32[2,4]{1,0:T(2,128)S(1)} copy-done((s32[2,4]{1,0:T(2,128)S(1)}, s32[2,4]{1,0:T(2,128)}, u32[]{:S(2)}) %copy-start.2) | copy-done | bytes 56
  2.3 50.4 %shard_map.37 = bf16[256,512]{1,0:T(8,128)(2,1)S(1)} custom-call(bf16[256,512]{1,0:T(8,128)(2,1)S(1)} %copy-done, s32[2,4]{1,0:T(2,128)S(1)} %copy-done.1, s32[2,4]{1,0:T(2,128)S(1)} %copy-done.2), custom_call_target="tpu_custom_call" | custom-call | tf_op jit(solution)/shard_map/pallas_call | solution.py:448
  52.7 0.7 %copy.5 = bf16[256,512]{1,0:T(8,128)(2,1)} copy(bf16[256,512]{1,0:T(8,128)(2,1)S(1)} %shard_map.37) | data formatting | bytes 524288
Async XLA Ops:
  0.0 0.9 %copy-start = (bf16[256,512]{1,0:T(8,128)(2,1)S(1)}, bf16[256,512]{1,0:T(8,128)(2,1)}, u32[]{:S(2)}) copy-start(bf16[256,512]{1,0:T(8,128)(2,1)} %w_hbm.1) | copy-start | bytes 786436
  1.0 0.7 %copy-start.1 = (s32[2,4]{1,0:T(2,128)S(1)}, s32[2,4]{1,0:T(2,128)}, u32[]{:S(2)}) copy-start(s32[2,4]{1,0:T(2,128)} %ip_hbm.1) | copy-start | bytes 100
  1.6 0.7 %copy-start.2 = (s32[2,4]{1,0:T(2,128)S(1)}, s32[2,4]{1,0:T(2,128)}, u32[]{:S(2)}) copy-start(s32[2,4]{1,0:T(2,128)} %op_hbm.1) | copy-start | bytes 100

commit v6 on v5

--- a/solution.py
+++ b/solution.py
@@ -13,7 +13,7 @@
 CAP = 4
 CODE = 16
 P_ROWS = 192
-ROW, HOP, START, TAKE = 5.5e-3, 2.4, 0.08, 0.05
+ROW, HOP, START, TAKE = 6.2e-3, 3.0, 0.1, 0.06
 
 ALL = 2
 RELAYS = 3
@@ -182,12 +182,6 @@
     def at_y(dy, c):
         return lax.rem(y + (dy + y_chips), y_chips) * CORES + c
 
-    loads = [
-        pltpu.make_async_copy(src, dst, local_sem.at[i])
-        for i, (src, dst) in enumerate(((ip_hbm, ip_ref), (w_hbm, w_ref), (op_hbm, op_ref)))
-    ]
-    for load in loads:
-        load.start()
     barrier = pltpu.get_barrier_semaphore()
     x_peers = [{"gc": at(i, 0)} for i in range(1, X)]
     z_peers = [{"gc": at(0, i)} for i in range(1, z_chips)]
@@ -197,7 +191,13 @@
     greeted = nearest + [other_core]
     for peer in greeted:
         pl.semaphore_signal(barrier, inc=1, device_id=peer, device_id_type=MESH)
+    loads = [
+        pltpu.make_async_copy(src, dst, local_sem.at[i])
+        for i, (src, dst) in enumerate(((w_hbm, w_ref), (ip_hbm, ip_ref), (op_hbm, op_ref)))
+    ]
     for load in loads:
+        load.start()
+    for load in loads[:2]:
         load.wait()
 
     spots = br * bc
@@ -220,12 +220,6 @@
         r, c = p // bc, p % bc
         return w_ref[r * blk : (r + 1) * blk, c * blk : (c + 1) * blk]
 
-    for c in range(bc):
-        total = jnp.zeros((1, blk), f32)
-        for r in range(br):
-            block = block_of(r * bc + c).astype(f32)
-            total += jnp.sum(block, axis=0, keepdims=True) * on[r * bc + c].astype(f32)
-        x_sums[0, c : c + 1, :] = total
     def put(first, block):
         size = block.shape[0]
         abuf[0, first : first + size, :] = block
@@ -355,6 +349,13 @@
     for step in first_copies(z_chips):
         link(*step).start()
     sib_copy(0).start()
+
+    for c in range(bc):
+        total = jnp.zeros((1, blk), f32)
+        for r in range(br):
+            block = block_of(r * bc + c).astype(f32)
+            total += jnp.sum(block, axis=0, keepdims=True) * on[r * bc + c].astype(f32)
+        x_sums[0, c : c + 1, :] = total
 
     taken = set()
     first = True
@@ -404,6 +405,7 @@
             first = False
         taken.add(step)
 
+    loads[2].wait()
     for c in range(bc):
         total = jnp.zeros((1, blk), f32)
         for r in range(br):

time: 53.6 us -> 52.9 us (0.987)
  Pallas kernels: 50.4 us -> 49.7 us
    pallas_call x1, Pallas kernels: 50.4 us -> 49.7 us  [shards(): pl.pallas_call(functools.partial(kernel, gc, gr, blk), out_shape=jax.Shap...]
where the time goes in v6:
time: 52.9 us; the launch traced here: 52.7 us
  Pallas kernels  49.7 us (94%)
  local copies, waits for them, and re-layouts  3.01 us (6%)
    pallas_call x1, Pallas kernels, shards(): pl.pallas_call(functools.partial(kernel, gc, gr, blk), out_shape=jax.Shap...  49.7 us
    unnamed x7, local copies, waits for them, and re-layouts  3.01 us

profile of v6, /device:TPU:24, one launch (start us, length us, event | category | flops | bytes accessed | tf_op | source)
XLA Modules:
  0.0 52.7 jit_solution(14241599716684581049)
XLA Ops:
  0.0 0.0 copy-start
  0.0 0.9 %copy-done = bf16[256,512]{1,0:T(8,128)(2,1)S(1)} copy-done((bf16[256,512]{1,0:T(8,128)(2,1)S(1)}, bf16[256,512]{1,0:T(8,128)(2,1)}, u32[]{:S(2)}) %copy-start) | copy-done | bytes 262168
  1.0 0.0 copy-start.1
  1.0 0.7 %copy-done.1 = s32[2,4]{1,0:T(2,128)S(1)} copy-done((s32[2,4]{1,0:T(2,128)S(1)}, s32[2,4]{1,0:T(2,128)}, u32[]{:S(2)}) %copy-start.1) | copy-done | bytes 56
  1.6 0.0 copy-start.2
  1.6 0.7 %copy-done.2 = s32[2,4]{1,0:T(2,128)S(1)} copy-done((s32[2,4]{1,0:T(2,128)S(1)}, s32[2,4]{1,0:T(2,128)}, u32[]{:S(2)}) %copy-start.2) | copy-done | bytes 56
  2.3 49.7 %shard_map.37 = bf16[256,512]{1,0:T(8,128)(2,1)S(1)} custom-call(bf16[256,512]{1,0:T(8,128)(2,1)S(1)} %copy-done, s32[2,4]{1,0:T(2,128)S(1)} %copy-done.1, s32[2,4]{1,0:T(2,128)S(1)} %copy-done.2), custom_call_target="tpu_custom_call" | custom-call | tf_op jit(solution)/shard_map/pallas_call | solution.py:450
  52.0 0.7 %copy.5 = bf16[256,512]{1,0:T(8,128)(2,1)} copy(bf16[256,512]{1,0:T(8,128)(2,1)S(1)} %shard_map.37) | data formatting | bytes 524288
Async XLA Ops:
  0.0 0.9 %copy-start = (bf16[256,512]{1,0:T(8,128)(2,1)S(1)}, bf16[256,512]{1,0:T(8,128)(2,1)}, u32[]{:S(2)}) copy-start(bf16[256,512]{1,0:T(8,128)(2,1)} %w_hbm.1) | copy-start | bytes 786436
  1.0 0.7 %copy-start.1 = (s32[2,4]{1,0:T(2,128)S(1)}, s32[2,4]{1,0:T(2,128)}, u32[]{:S(2)}) copy-start(s32[2,4]{1,0:T(2,128)} %ip_hbm.1) | copy-start | bytes 100
  1.6 0.7 %copy-start.2 = (s32[2,4]{1,0:T(2,128)S(1)}, s32[2,4]{1,0:T(2,128)}, u32[]{:S(2)}) copy-start(s32[2,4]{1,0:T(2,128)} %op_hbm.1) | copy-start | bytes 100

commit v7 on v6

--- a/solution.py
+++ b/solution.py
@@ -66,7 +66,7 @@
 
 def plan(z_chips, y_chips, tile):
     row, hop, start, take = ROW, HOP, START, TAKE
-    spread, dot, left = 0.5, 0.4, 0.25
+    spread, dot, left = 0.7, 0.6, 0.4
     z_half, x_half, y_half = z_chips // 2, X // 2, y_chips // 2
     Q, PX = X, z_chips
     now, serial, free, arrivals, steps, done = 0.0, 0, {}, [], [], set()

time: 52.9 us -> 53.8 us (1.017)
  Pallas kernels: 49.7 us -> 50.6 us
    pallas_call x1, Pallas kernels: 49.7 us -> 50.6 us  [shards(): pl.pallas_call(functools.partial(kernel, gc, gr, blk), out_shape=jax.Shap...]
where the time goes in v7:
time: 53.8 us; the launch traced here: 53.6 us
  Pallas kernels  50.6 us (94%)
  local copies, waits for them, and re-layouts  3.01 us (6%)
    pallas_call x1, Pallas kernels, shards(): pl.pallas_call(functools.partial(kernel, gc, gr, blk), out_shape=jax.Shap...  50.6 us
    unnamed x7, local copies, waits for them, and re-layouts  3.01 us

profile of v7, /device:TPU:24, one launch (start us, length us, event | category | flops | bytes accessed | tf_op | source)
XLA Modules:
  0.0 53.6 jit_solution(14425113795173755589)
XLA Ops:
  0.0 0.0 copy-start
  0.0 0.9 %copy-done = bf16[256,512]{1,0:T(8,128)(2,1)S(1)} copy-done((bf16[256,512]{1,0:T(8,128)(2,1)S(1)}, bf16[256,512]{1,0:T(8,128)(2,1)}, u32[]{:S(2)}) %copy-start) | copy-done | bytes 262168
  1.0 0.0 copy-start.1
  1.0 0.7 %copy-done.1 = s32[2,4]{1,0:T(2,128)S(1)} copy-done((s32[2,4]{1,0:T(2,128)S(1)}, s32[2,4]{1,0:T(2,128)}, u32[]{:S(2)}) %copy-start.1) | copy-done | bytes 56
  1.6 0.0 copy-start.2
  1.6 0.7 %copy-done.2 = s32[2,4]{1,0:T(2,128)S(1)} copy-done((s32[2,4]{1,0:T(2,128)S(1)}, s32[2,4]{1,0:T(2,128)}, u32[]{:S(2)}) %copy-start.2) | copy-done | bytes 56
  2.3 50.6 %shard_map.37 = bf16[256,512]{1,0:T(8,128)(2,1)S(1)} custom-call(bf16[256,512]{1,0:T(8,128)(2,1)S(1)} %copy-done, s32[2,4]{1,0:T(2,128)S(1)} %copy-done.1, s32[2,4]{1,0:T(2,128)S(1)} %copy-done.2), custom_call_target="tpu_custom_call" | custom-call | tf_op jit(solution)/shard_map/pallas_call | solution.py:450
  52.9 0.7 %copy.5 = bf16[256,512]{1,0:T(8,128)(2,1)} copy(bf16[256,512]{1,0:T(8,128)(2,1)S(1)} %shard_map.37) | data formatting | bytes 524288
Async XLA Ops:
  0.0 0.9 %copy-start = (bf16[256,512]{1,0:T(8,128)(2,1)S(1)}, bf16[256,512]{1,0:T(8,128)(2,1)}, u32[]{:S(2)}) copy-start(bf16[256,512]{1,0:T(8,128)(2,1)} %w_hbm.1) | copy-start | bytes 786436
  1.0 0.7 %copy-start.1 = (s32[2,4]{1,0:T(2,128)S(1)}, s32[2,4]{1,0:T(2,128)}, u32[]{:S(2)}) copy-start(s32[2,4]{1,0:T(2,128)} %ip_hbm.1) | copy-start | bytes 100
  1.6 0.7 %copy-start.2 = (s32[2,4]{1,0:T(2,128)S(1)}, s32[2,4]{1,0:T(2,128)}, u32[]{:S(2)}) copy-start(s32[2,4]{1,0:T(2,128)} %op_hbm.1) | copy-start | bytes 100
